TPU v7x, 32 devices: a whole 2x2x4 slice. The times are simulated.
32 devices in a mesh: dp: 8 (over z, x), mp: 4 (over y, core).
Axes of the slice: x: 2, y: 2, z: 4, core: 2. Of those that a mesh axis runs over, the one named last changes fastest.
Arguments:
- images: bfloat16 [128, 196, 512], P('dp'), may hold values from -6 to 6
- cotangent: bfloat16 [128, 196, 512], P('dp'), may hold values from -6 to 6
- qkv_weight: float32 [1536, 512], P(('mp', 'dp')), may hold values from -0.25 to 0.25
- proj_weight: float32 [512, 512], P(('mp', 'dp')), may hold values from -0.5 to 0.5
- expand_weight: float32 [2048, 512], P(('mp', 'dp')), may hold values from -0.25 to 0.25
- contract_weight: float32 [2048, 512], P(('mp', 'dp')), may hold values from -0.125 to 0.125
- qkv_moment: float32 [1536, 512], P(('mp', 'dp')), may hold values from -256 to 256
- proj_moment: float32 [512, 512], P(('mp', 'dp')), may hold values from -256 to 256
- expand_moment: float32 [2048, 512], P(('mp', 'dp')), may hold values from -192 to 192
- contract_moment: float32 [2048, 512], P(('mp', 'dp')), may hold values from -384 to 384
- vectors: float32 [6, 512], replicated, may hold values from -1.2 to 2.2
- qv_bias: float32 [2, 512], P(None, 'mp'), may hold values from -3 to 3
- expand_bias: float32 [2048], P('mp'), may hold values from -3 to 3
- rel_table: float32 [169, 16], P(None, 'mp'), may hold values from -3 to 334
- vectors_first: float32 [6, 512], replicated, may hold values from -80 to 80
- vectors_second: float32 [6, 512], replicated, may hold values from 7.5264 to 30.1056
- qv_first: float32 [2, 512], P(None, 'mp'), may hold values from -40 to 40
- qv_second: float32 [2, 512], P(None, 'mp'), may hold values from 2.5088 to 10.0352
- expand_bias_first: float32 [2048], P('mp'), may hold values from -20 to 20
- expand_bias_second: float32 [2048], P('mp'), may hold values from 0.75264 to 2.5088
- table_first: float32 [169, 16], P(None, 'mp'), may hold values from -6 to 6
- table_second: float32 [169, 16], P(None, 'mp'), may hold values from 0.0075264 to 0.0301056
- region_ids: int32 [14, 14], replicated, may hold values from 0 to 3
- pos_index: int32 [49, 49], replicated, may hold values from 0 to 168
- image_counts: int32 [8], P('dp'), may hold values from 1 to 16, as said below
Outputs:
- block_out: bfloat16 [128, 196, 512], P('dp')
- input_grad: bfloat16 [128, 196, 512], P('dp')
- qkv_grad: float32 [1536, 512], P(('mp', 'dp'))
- proj_grad: float32 [512, 512], P(('mp', 'dp'))
- expand_grad: float32 [2048, 512], P(('mp', 'dp'))
- contract_grad: float32 [2048, 512], P(('mp', 'dp'))
- vectors_grad: float32 [6, 512], replicated
- qv_grad: float32 [2, 512], P(None, 'mp')
- expand_bias_grad: float32 [2048], P('mp')
- table_grad: float32 [169, 16], P(None, 'mp')
- qkv_step: float32 [1536, 512], P(('mp', 'dp'))
- proj_step: float32 [512, 512], P(('mp', 'dp'))
- expand_step: float32 [2048, 512], P(('mp', 'dp'))
- contract_step: float32 [2048, 512], P(('mp', 'dp'))
- qkv_moment_new: float32 [1536, 512], P(('mp', 'dp'))
- proj_moment_new: float32 [512, 512], P(('mp', 'dp'))
- expand_moment_new: float32 [2048, 512], P(('mp', 'dp'))
- contract_moment_new: float32 [2048, 512], P(('mp', 'dp'))
- vectors_step: float32 [6, 512], replicated
- qv_step: float32 [2, 512], P(None, 'mp')
- expand_bias_step: float32 [2048], P('mp')
- table_step: float32 [169, 16], P(None, 'mp')
- vectors_first_new: float32 [6, 512], replicated
- vectors_second_new: float32 [6, 512], replicated
- qv_first_new: float32 [2, 512], P(None, 'mp')
- qv_second_new: float32 [2, 512], P(None, 'mp')
- expand_bias_first_new: float32 [2048], P('mp')
- expand_bias_second_new: float32 [2048], P('mp')
- table_first_new: float32 [169, 16], P(None, 'mp')
- table_second_new: float32 [169, 16], P(None, 'mp')
Inputs may be any that keep to these rules, and one draw needn't show every extreme that they name: `image_counts`: some index of dp has all 16 images live.
All inputs are finite; a program needn't handle non-finite values.
Results may differ from a plain program's by a relative error of at most 0.018.
The roundings to bfloat16 on the way count: a program that leaves them out, or rounds other values in their place, can miss the bound.
Values may be sent and summed in bfloat16 or wider, within the bound.
A program may use at most 192 MiB of HBM per device.

v0:
```python
import functools
import math

import jax
import jax.numpy as jnp
import numpy as np
from jax import lax
from jax.experimental import pallas as pl
from jax.experimental.pallas import tpu as pltpu
from jax.sharding import PartitionSpec as P

C = 512
HEADS = 16
HD = 32
FF = 2048
WIN = 7
SIDE = 14
SHIFT = 3
SPAN = WIN * WIN
TOK = SIDE * SIDE
NS_ITERS = 5
IMG_DEV = 16
TABLE = 169
PAIR = 112
ROWS = 2 * PAIR
GROUP = 4

norm_eps = 1e-05
ns_eps = 1e-07
coef_a = 3.4445
coef_b = -4.775
coef_c = 2.0315
muon_rate = 0.3
muon_decay = 0.1
muon_beta = 0.95
adam_rate = 0.1
adam_one = 0.9
adam_two = 0.999
adam_eps = 1e-08
adam_step = 4
mask_value = -100.0
away = -1e30
wide = jnp.float32
low = jnp.bfloat16
highest = lax.Precision.HIGHEST


def to_windows(field_values):
    image_total = field_values.shape[0]
    channels = field_values.shape[-1]
    blocks = SIDE // WIN
    grid_values = field_values.reshape(image_total, SIDE, SIDE, channels)
    grid_values = jnp.roll(grid_values, (-SHIFT, -SHIFT), axis=(1, 2))
    grid_values = grid_values.reshape(image_total, blocks, WIN, blocks, WIN, channels)
    grid_values = grid_values.transpose(0, 1, 3, 2, 4, 5)
    return grid_values.reshape(image_total * blocks * blocks, WIN * WIN, channels)


def window_order():
    order = np.full((ROWS,), -1, np.int64)
    for window in range(4):
        top, left = window // 2, window % 2
        for token in range(SPAN):
            row = (top * WIN + token // WIN + SHIFT) % SIDE
            column = (left * WIN + token % WIN + SHIFT) % SIDE
            order[(window // 2) * PAIR + (window % 2) * SPAN + token] = row * SIDE + column
    return order


def dot(a, b):
    return jnp.dot(a, b, preferred_element_type=wide)


def dot_nt(a, b):
    return lax.dot_general(a, b, (((1,), (1,)), ((), ())), preferred_element_type=wide)


def dot_tn(a, b):
    return lax.dot_general(a, b, (((0,), (0,)), ((), ())), preferred_element_type=wide)


def mean_of(values):
    return jnp.sum(values, axis=-1, keepdims=True) * (1.0 / C)


def normalize(values):
    centered = values - mean_of(values)
    inv_scale = lax.rsqrt(mean_of(centered * centered) + norm_eps)
    return centered * inv_scale, inv_scale


def normalize_back(grad_norm, normed, inv_scale, gain):
    scaled = grad_norm * gain
    return inv_scale * (scaled - mean_of(scaled) - normed * mean_of(scaled * normed))


def column_sum(values):
    return jnp.sum(values, axis=0, keepdims=True)


def head_masks():
    lane = lax.broadcasted_iota(jnp.int32, (1, 128), 1) // HD
    return [(lane == head).astype(wide).astype(low) for head in range(GROUP)]


def stack_heads(block, masks):
    return jnp.concatenate([block * mask for mask in masks], axis=0)


def pick_heads(stacked):
    lane = lax.broadcasted_iota(jnp.int32, (PAIR, 128), 1)
    parts = [stacked[PAIR * head : PAIR * (head + 1)] for head in range(GROUP)]
    return jnp.where(
        lane < 2 * HD,
        jnp.where(lane < HD, parts[0], parts[1]),
        jnp.where(lane < 3 * HD, parts[2], parts[3]),
    )


def layer_kernel(
    packed, batch, place, images, cotangent, order, order_back, vectors, qv_bias, expand_bias, bias,
    qkv_hbm, proj_hbm, expand_hbm, contract_hbm,
    block_out, input_grad, *rest,
):
    n_grads = 1 if packed else 4
    grad_outs = rest[:n_grads]
    (small, table_sum, qkv_nat, qkv_w, proj_w, expand_w, contract_w,
     qkv_acc, proj_acc, expand_acc, contract_acc,
     qkv_s, att_s, back_s, probs_s, normed_s, first_s, middle_s, normed2_s, second_s,
     out_low_s, mlp_s, second_grad_s, sems) = rest[n_grads : n_grads + 24]
    step = pl.program_id(0)
    steps = pl.num_programs(0)
    masks = head_masks()
    if packed:
        staged, keep_sem, act_send, act_recv = rest[n_grads + 24 :]
        at = Place()
        per_device = staged.shape[0]
        over = (1 - at.y) * 2 + at.core
        across = (1 - at.y) * 2 + 1 - at.core
        beside = at.y * 2 + 1 - at.core

        def slot(mp_index, image):
            return block_out.at[mp_index * per_device + image]

        def keep_copy(image):
            return pltpu.make_async_copy(staged.at[image], slot(at.mp_index, image), keep_sem.at[image])

        def own_copy(which, image):
            device = (at.partner, at.y_side)[which]
            return remote(
                staged.at[image], slot(at.mp_index, image),
                act_send.at[which, image], act_recv.at[which, image], device,
            )

        def own_arrival(which, image):
            source, device = ((beside, at.partner), (over, at.y_side))[which]
            return remote(
                staged.at[image], slot(source, image),
                act_send.at[which, image], act_recv.at[which, image], device,
            )

        def relay(image):
            return remote(
                slot(over, image), slot(over, image), act_send.at[2, image], act_recv.at[2, image], at.partner
            )

        def relay_arrival(image):
            return remote(
                slot(across, image), slot(across, image), act_send.at[2, image], act_recv.at[2, image], at.partner
            )

        def pass_on(of_step):
            for slice_ in range(batch):
                image = of_step * batch + slice_
                own_arrival(1, image).wait_recv()
                relay(image).start()

        def greet():
            barrier = pltpu.get_barrier_semaphore()
            for device in (at.partner, at.y_side):
                pl.semaphore_signal(barrier, inc=1, device_id=device, device_id_type=MESH)
            pl.semaphore_wait(barrier, 2)

        pl.when(step == 0)(greet)

    def put_block(slice_, value):
        if packed:
            image = step * batch + slice_
            staged[image] = value
            own_copy(1, image).start()
            own_copy(0, image).start()
            keep_copy(image).start()
        else:
            block_out[slice_] = value

    def put_grad(slice_, value):
        input_grad[slice_] = value

    row = lax.broadcasted_iota(jnp.int32, (batch * ROWS, 1), 0) // ROWS
    live_scale = jnp.zeros((batch * ROWS, 1), wide)
    for slice_ in range(batch):
        is_live = (place[1] > place[0] + step * batch + slice_).astype(wide)
        live_scale = jnp.where(row == slice_, is_live, live_scale)

    def fetch(which):
        if packed:
            counts = (48, 16, 64, 64)
            source = qkv_hbm.at[:, pl.ds(sum(counts[:which]), counts[which])]
            target = (qkv_nat, proj_w, expand_w, contract_w)[which]
        else:
            source = (qkv_hbm, proj_hbm, expand_hbm, contract_hbm)[which]
            target = (qkv_nat, proj_w, expand_w, contract_w)[which]
        return pltpu.make_async_copy(source, target, sems.at[which])

    def rows_of(ref, count):
        return ref[...].reshape(count, C)

    def begin():
        for which in range(4):
            fetch(which).start()
        for ref in (qkv_acc, proj_acc, expand_acc, contract_acc, small, table_sum):
            ref[...] = jnp.zeros_like(ref)
        for which in range(4):
            fetch(which).wait()
        natural = rows_of(qkv_nat, 3 * C).reshape(HEADS, 3, HD, C)
        for kind in range(3):
            qkv_w[kind] = natural[:, kind].reshape(C, C)

    pl.when(step == 0)(begin)

    tokens = jnp.concatenate([dot(order[...], images[slice_]) for slice_ in range(batch)], axis=0)
    normed, inv_one = normalize(tokens)
    normed_s[...] = normed
    first_in = (normed * vectors[0:1] + vectors[1:2]).astype(low)
    first_s[...] = first_in
    for kind in range(3):
        projected = dot_nt(first_in, qkv_w[kind])
        if kind != 1:
            projected = projected + qv_bias[kind // 2 : kind // 2 + 1]
        projected = projected.astype(low)
        for group in range(4):
            qkv_s[kind * 4 + group] = projected[:, 128 * group : 128 * (group + 1)]
    score_scale = 1.0 / math.sqrt(HD)

    def attend(which, carry):
        pair, group = which // 4, which % 4
        pair_scores = bias[pair, group]
        for slice_ in range(batch):
            rows = pl.ds(pl.multiple_of(slice_ * ROWS + pair * PAIR, 16), PAIR)
            queries = stack_heads(qkv_s[group, rows], masks)
            scores = dot_nt(queries, qkv_s[4 + group, rows]) * score_scale + pair_scores
            top = jnp.max(scores, axis=-1, keepdims=True)
            exponent = jnp.exp(scores - top)
            attention = exponent / jnp.sum(exponent, axis=-1, keepdims=True)
            probs_s[slice_, which] = attention
            att_s[group, rows] = pick_heads(dot(attention.astype(low), qkv_s[8 + group, rows])).astype(low)
        return carry

    lax.fori_loop(0, 8, attend, 0)
    attended = jnp.concatenate([att_s[group] for group in range(4)], axis=1)
    middle = tokens + (dot(attended, rows_of(proj_w, C)) + vectors[4:5])
    middle_s[...] = middle
    normed_two, inv_two = normalize(middle)
    normed2_s[...] = normed_two
    second_in = (normed_two * vectors[2:3] + vectors[3:4]).astype(low)
    second_s[...] = second_in

    grad_tokens = jnp.concatenate([dot(order[...], cotangent[slice_]) for slice_ in range(batch)], axis=0)
    out_low = (grad_tokens * live_scale).astype(low)
    out_low_s[...] = out_low
    mlp_s[...] = jnp.zeros_like(mlp_s)
    second_grad_s[...] = jnp.zeros_like(second_grad_s)
    chunk = 512
    owners = expand_w.shape[0] // (FF // chunk)

    def feed(which, carry):
        units = pl.ds(pl.multiple_of(which * owners, owners), owners)
        expand_part = expand_w[units].reshape(chunk, C)
        contract_part = contract_w[units].reshape(chunk, C)
        second = second_s[...]
        grad_rows = out_low_s[...]
        hidden = dot_nt(second, expand_part) + expand_bias[which]
        cumulative = 0.5 * (1.0 + lax.erf(hidden * (1.0 / math.sqrt(2.0))))
        acted = (hidden * cumulative).astype(low)
        slope = cumulative + hidden * jnp.exp(-0.5 * hidden * hidden) * (1.0 / math.sqrt(2.0 * math.pi))
        mlp_s[...] += dot(acted, contract_part)
        hidden_grad32 = dot_nt(grad_rows, contract_part) * slope
        hidden_grad = hidden_grad32.astype(low)
        small[pl.ds(8 + which, 1)] += column_sum(hidden_grad.astype(wide))
        second_grad_s[...] += dot(hidden_grad, expand_part)
        units_wide = pl.ds(pl.multiple_of(which * chunk, chunk), chunk)
        contract_acc[units_wide] += dot_tn(acted, grad_rows)
        expand_acc[units_wide] += dot_tn(hidden_grad, second)
        return carry

    lax.fori_loop(0, FF // chunk, feed, 0)
    result = middle_s[...] + (mlp_s[...] + vectors[5:6])
    result = jnp.where(live_scale > 0.0, result, 0.0).astype(low)
    if packed:
        pl.when(step > 0)(lambda: pass_on(step - 1))
    for slice_ in range(batch):
        put_block(slice_, dot(order_back[...], result[ROWS * slice_ : ROWS * (slice_ + 1)]).astype(low))

    grad_out = out_low_s[...].astype(wide)
    second_grad = second_grad_s[...]
    normed_two = normed2_s[...]
    small[5:6] += column_sum(grad_out)
    small[3:4] += column_sum(second_grad)
    small[2:3] += column_sum(second_grad * normed_two)
    middle_grad = grad_out + normalize_back(second_grad, normed_two, inv_two, vectors[2:3])
    small[4:5] += column_sum(middle_grad)
    middle_s[...] = middle_grad
    attn_low = middle_grad.astype(low)
    attended = jnp.concatenate([att_s[group] for group in range(4)], axis=1)
    proj_acc[...] += dot_tn(attended, attn_low)
    attended_grad = dot_nt(attn_low, rows_of(proj_w, C)).astype(low)
    for group in range(4):
        att_s[group] = attended_grad[:, 128 * group : 128 * (group + 1)]

    def attend_back(which, carry):
        pair, group = which // 4, which % 4
        bias_grad = None
        for slice_ in range(batch):
            rows = pl.ds(pl.multiple_of(slice_ * ROWS + pair * PAIR, 16), PAIR)
            attention = probs_s[slice_, which]
            keys, values = qkv_s[4 + group, rows], qkv_s[8 + group, rows]
            grads = stack_heads(att_s[group, rows], masks)
            queries = stack_heads(qkv_s[group, rows], masks)
            probs_grad = dot_nt(grads, values)
            row_term = jnp.sum(attention * probs_grad, axis=-1, keepdims=True)
            score_grad = (attention * (probs_grad - row_term)).astype(low)
            wide_grad = score_grad.astype(wide)
            bias_grad = wide_grad if bias_grad is None else bias_grad + wide_grad
            back_s[group, rows] = (pick_heads(dot(score_grad, keys)) * score_scale).astype(low)
            back_s[4 + group, rows] = (dot_tn(score_grad, queries) * score_scale).astype(low)
            back_s[8 + group, rows] = dot_tn(attention.astype(low), grads).astype(low)
        table_sum[group] += bias_grad
        return carry

    lax.fori_loop(0, 8, attend_back, 0)
    first_in = first_s[...]
    first_grad = None
    for kind in range(3):
        back = jnp.concatenate([back_s[kind * 4 + group] for group in range(4)], axis=1)
        if kind != 1:
            row = 6 + kind // 2
            small[row : row + 1] += column_sum(back.astype(wide))
        qkv_acc[kind] += dot_tn(back, first_in)
        part = dot(back, qkv_w[kind])
        first_grad = part if first_grad is None else first_grad + part
    normed = normed_s[...]
    small[1:2] += column_sum(first_grad)
    small[0:1] += column_sum(first_grad * normed)
    token_grad = middle_s[...] + normalize_back(first_grad, normed, inv_one, vectors[0:1])
    token_low = token_grad.astype(low)
    for slice_ in range(batch):
        put_grad(slice_, dot(order_back[...], token_low[ROWS * slice_ : ROWS * (slice_ + 1)]).astype(low))

    def finish():
        if packed:
            pass_on(steps - 1)
        for kind in range(3):
            part = qkv_acc[kind].astype(low).reshape(HEADS, HD, C)
            if packed:
                out = grad_outs[0]
                for piece in range(2):
                    block = kind * 2 + piece
                    out[:, block // 3, pl.ds(16 * (block % 3), 16)] = part[:, 16 * piece : 16 * (piece + 1)]
            else:
                grad_outs[0][:, kind] = part
        if packed:
            out = grad_outs[0]
            out[:, :, pl.ds(48, 16)] = proj_acc[...].astype(low).reshape(16, 2, 16, C)
            out[:, :, pl.ds(64, 64)] = expand_acc[...].astype(low).reshape(16, 2, 64, C)
            out[:, :, pl.ds(128, 64)] = contract_acc[...].astype(low).reshape(16, 2, 64, C)
        else:
            grad_outs[1][...] = proj_acc[...].astype(low)
            grad_outs[2][...] = expand_acc[...].astype(low)
            grad_outs[3][...] = contract_acc[...].astype(low)
        if packed:

            def settle(image, carry):
                own_arrival(0, image).wait_recv()
                relay_arrival(image).wait_recv()
                own_copy(0, image).wait_send()
                own_copy(1, image).wait_send()
                relay(image).wait_send()
                keep_copy(image).wait()
                return carry

            lax.fori_loop(0, per_device, settle, 0)

    pl.when(step == steps - 1)(finish)


def run_layer(packed, per_device, place, images, cotangent, vectors, qv_bias, expand_bias, bias, weights):
    order_np = window_order()
    onehot = (order_np[:, None] == np.arange(TOK)[None, :]).astype(np.float32)
    order = jnp.asarray(onehot, low)
    order_back = jnp.asarray(onehot.T, low)
    any_spec = pl.BlockSpec(memory_space=pl.ANY)

    def whole(shape):
        return pl.BlockSpec(shape, lambda i, s: (0,) * len(shape), pipeline_mode=pl.Buffered(1))

    batch = 2 if per_device % 2 == 0 else 1
    span = batch * ROWS
    image_spec = pl.BlockSpec((batch, TOK, C), lambda i, s: (i, 0, 0))
    out_spec = any_spec if packed else image_spec
    images_out = IMG_DEV if packed else per_device
    exchange = [
        pltpu.VMEM((per_device, TOK, C), low),
        pltpu.SemaphoreType.DMA((per_device,)),
        pltpu.SemaphoreType.DMA((3, per_device)),
        pltpu.SemaphoreType.DMA((3, per_device)),
    ]
    limit = 60 * 1024 * 1024
    if packed:
        params = pltpu.CompilerParams(collective_id=3, has_side_effects=True, vmem_limit_bytes=limit)
    else:
        params = pltpu.CompilerParams(vmem_limit_bytes=limit)
    if packed:
        weights = (weights,) * 4
        grad_shapes = [(16, 2, 192, C)]
        weight_shapes = [(32, 48, C), (32, 16, C), (32, 64, C), (32, 64, C)]
    else:
        weights = (weights[0], weights[1], weights[2].reshape(FF // 64, 64, C), weights[3].reshape(FF // 64, 64, C))
        grad_shapes = [(HEADS, 3, HD, C), (C, C), (FF, C), (FF, C)]
        weight_shapes = [w.shape for w in weights]
    outs = pl.pallas_call(
        functools.partial(layer_kernel, packed, batch),
        out_shape=[
            jax.ShapeDtypeStruct((images_out, TOK, C), low),
            jax.ShapeDtypeStruct((per_device, TOK, C), low),
            *[jax.ShapeDtypeStruct(shape, low) for shape in grad_shapes],
            jax.ShapeDtypeStruct((16, C), wide),
            jax.ShapeDtypeStruct((4, GROUP * PAIR, PAIR), wide),
        ],
        grid_spec=pltpu.PrefetchScalarGridSpec(
            num_scalar_prefetch=1,
            grid=(per_device // batch,),
            in_specs=[
                image_spec, image_spec, whole((ROWS, TOK)), whole((TOK, ROWS)), whole((6, C)), whole((2, C)),
                whole((4, 1, C)), whole((2, 4, GROUP * PAIR, PAIR)), any_spec, any_spec, any_spec, any_spec,
            ],
            out_specs=[out_spec, image_spec]
            + [whole(shape) for shape in grad_shapes]
            + [whole((16, C)), whole((4, GROUP * PAIR, PAIR))],
            scratch_shapes=[pltpu.VMEM(shape, low) for shape in weight_shapes[:1]]
            + [pltpu.VMEM((3, C, C), low)]
            + [pltpu.VMEM(shape, low) for shape in weight_shapes[1:]]
            + [
                pltpu.VMEM((3, C, C), wide),
                pltpu.VMEM((C, C), wide),
                pltpu.VMEM((FF, C), wide),
                pltpu.VMEM((FF, C), wide),
                pltpu.VMEM((12, span, 128), low),
                pltpu.VMEM((4, span, 128), low),
                pltpu.VMEM((12, span, 128), low),
                pltpu.VMEM((batch, 8, GROUP * PAIR, PAIR), wide),
                pltpu.VMEM((span, C), wide),
                pltpu.VMEM((span, C), low),
                pltpu.VMEM((span, C), wide),
                pltpu.VMEM((span, C), wide),
                pltpu.VMEM((span, C), low),
                pltpu.VMEM((span, C), low),
                pltpu.VMEM((span, C), wide),
                pltpu.VMEM((span, C), wide),
                pltpu.SemaphoreType.DMA((4,)),
            ]
            + (exchange if packed else []),
        ),
        compiler_params=params,
        name="window_layer",
    )(place, images, cotangent, order, order_back, vectors, qv_bias, expand_bias.reshape(4, 1, C), bias, *weights)
    grads = outs[2 : 2 + len(grad_shapes)]
    grads = grads[0].reshape(32, 192, C) if packed else [g.reshape(-1, C) for g in grads]
    return outs[0], outs[1], grads, outs[-2], outs[-1]


def pair_bias(pos_bias, window_mask):
    heads = pos_bias.shape[0]
    scores = pos_bias[None] + window_mask[:, None]
    scores = scores.reshape(2, 2, heads, SPAN, SPAN)
    first = jnp.pad(scores[:, 0], ((0, 0), (0, 0), (0, 0), (0, PAIR - SPAN)), constant_values=away)
    second = jnp.pad(scores[:, 1], ((0, 0), (0, 0), (0, 0), (SPAN, PAIR - 2 * SPAN)), constant_values=away)
    rest = jnp.broadcast_to(
        jnp.where(jnp.arange(PAIR) < SPAN, 0.0, away).astype(wide), (2, heads, PAIR - 2 * SPAN, PAIR)
    )
    return jnp.concatenate([first, second, rest], axis=2).reshape(2, heads // GROUP, GROUP * PAIR, PAIR)


MESH = pl.DeviceIdType.MESH
DEPTH = 4


class Place:
    def __init__(self):
        dp_index, mp_index = lax.axis_index("dp"), lax.axis_index("mp")
        self.z, self.x = dp_index // 2, dp_index % 2
        self.y, self.core = mp_index // 2, mp_index % 2
        self.dp_index, self.mp_index = dp_index, mp_index
        self.x_side = self.device(self.z, 1 - self.x, self.y, self.core)
        self.y_side = self.device(self.z, self.x, 1 - self.y, self.core)
        self.partner = self.device(self.z, self.x, self.y, 1 - self.core)
        self.above = self.device(self.z + 1, self.x, self.y, self.core)
        self.below = self.device(self.z - 1, self.x, self.y, self.core)
        self.z_near = self.device(self.z + 1 - 2 * lax.rem(self.z, 2), self.x, self.y, self.core)
        self.z_far = self.device(lax.rem(self.z + 2, DEPTH), self.x, self.y, self.core)

    @staticmethod
    def device(z, x, y, core):
        return {"dp": z * 2 + x, "mp": y * 2 + core}

    @staticmethod
    def owner(z, x, y, core):
        return (y * 2 + core) * 8 + z * 2 + x

    def greet(self):
        barrier = pltpu.get_barrier_semaphore()

        def signal(device):
            pl.semaphore_signal(barrier, inc=1, device_id=device, device_id_type=MESH)

        signal(self.x_side)
        signal(self.y_side)
        signal(self.partner)
        pl.when(self.z > 0)(lambda: signal(self.below))
        pl.when(self.z < DEPTH - 1)(lambda: signal(self.above))
        ends = (self.z == 0).astype(jnp.int32) + (self.z == DEPTH - 1).astype(jnp.int32)
        pl.semaphore_wait(barrier, 5 - ends)


def remote(src, dst, send_sem, recv_sem, device):
    return pltpu.make_async_remote_copy(
        src_ref=src,
        dst_ref=dst,
        send_sem=send_sem,
        recv_sem=recv_sem,
        device_id=device,
        device_id_type=MESH,
    )


def spread(at, own_ref, out_ref, own_sem, z_send, z_recv, side_send, side_recv, pair_send, pair_recv):
    rows = own_ref.shape[0]
    half = rows // 2
    z, x, y, core = at.z, at.x, at.y, at.core
    low, high = pl.ds(0, half), pl.ds(half, rows - half)

    def slot(source_z, other_x, other_y):
        return out_ref.at[
            at.owner(source_z, 1 - x if other_x else x, 1 - y if other_y else y, core)
        ]

    def up(source_z, src=None):
        dst = slot(source_z, False, False)
        return remote(dst if src is None else src, dst, z_send.at[0, source_z], z_recv.at[0, source_z], at.above)

    def down(source_z, src=None):
        dst = slot(source_z, False, False)
        return remote(dst if src is None else src, dst, z_send.at[1, source_z], z_recv.at[1, source_z], at.below)

    def side(kind, source_z, src=None):
        if kind == 0 or kind == 1:
            dst = slot(source_z, False, False)
        elif kind == 2:
            dst = slot(source_z, True, False).at[low]
        else:
            dst = slot(source_z, False, True).at[high]
        device = at.x_side if kind in (0, 3) else at.y_side
        return remote(
            dst if src is None else src, dst, side_send.at[kind, source_z], side_recv.at[kind, source_z], device
        )

    def side_arrival(kind, source_z):
        if kind == 0:
            dst = slot(source_z, True, False)
        elif kind == 1:
            dst = slot(source_z, False, True)
        elif kind == 2:
            dst = slot(source_z, True, True).at[low]
        else:
            dst = slot(source_z, True, True).at[high]
        device = at.x_side if kind in (0, 3) else at.y_side
        return remote(dst, dst, side_send.at[kind, source_z], side_recv.at[kind, source_z], device)

    def pair_region(kind, source_z, of_core):
        other_x, other_y = ((False, False), (True, False), (False, True), (True, True), (True, True))[kind]
        ref = out_ref.at[at.owner(source_z, 1 - x if other_x else x, 1 - y if other_y else y, of_core)]
        if kind == 3:
            ref = ref.at[low]
        elif kind == 4:
            ref = ref.at[high]
        return ref

    def pair(kind, source_z, src=None):
        dst = pair_region(kind, source_z, core)
        return remote(
            dst if src is None else src, dst, pair_send.at[kind, source_z], pair_recv.at[kind, source_z], at.partner
        )

    def pair_arrival(kind, source_z):
        dst = pair_region(kind, source_z, 1 - core)
        return remote(dst, dst, pair_send.at[kind, source_z], pair_recv.at[kind, source_z], at.partner)

    keep = pltpu.make_async_copy(own_ref, slot(z, False, False), own_sem)
    pl.when(z < DEPTH - 1)(lambda: up(z, own_ref).start())
    pl.when(z > 0)(lambda: down(z, own_ref).start())
    side(0, z, own_ref).start()
    side(1, z, own_ref).start()
    pair(0, z, own_ref).start()
    keep.start()

    def plane(source_z):
        side_arrival(0, source_z).wait_recv()
        side(2, source_z).start()
        pair(1, source_z).start()
        side_arrival(1, source_z).wait_recv()
        side(3, source_z).start()
        pair(2, source_z).start()

    def column(source_z):
        side(0, source_z).start()
        side(1, source_z).start()
        pair(0, source_z).start()

    for distance in range(1, DEPTH + 1):

        def from_below(source_z=z - distance):
            up(source_z).wait_recv()
            pl.when(z < DEPTH - 1)(lambda: up(source_z).start())
            column(source_z)

        def from_above(source_z=z + distance):
            down(source_z).wait_recv()
            pl.when(z > 0)(lambda: down(source_z).start())
            column(source_z)

        pl.when(z - distance >= 0)(from_below)
        pl.when(z + distance <= DEPTH - 1)(from_above)
        past = distance - 1
        if past == 0:
            plane(z)
        else:
            pl.when(z - past >= 0)(functools.partial(plane, z - past))
            pl.when(z + past <= DEPTH - 1)(functools.partial(plane, z + past))

    def corner(source_z):
        side_arrival(2, source_z).wait_recv()
        pair(3, source_z).start()
        side_arrival(3, source_z).wait_recv()
        pair(4, source_z).start()

    for distance in range(DEPTH):
        if distance == 0:
            corner(z)
        else:
            pl.when(z - distance >= 0)(functools.partial(corner, z - distance))
            pl.when(z + distance <= DEPTH - 1)(functools.partial(corner, z + distance))
    keep.wait()
    for source_z in range(DEPTH):
        for kind in range(5):
            pair_arrival(kind, source_z).wait_recv()
            pair(kind, source_z).wait_send()
        for kind in range(4):
            side(kind, source_z).wait_send()
        pl.when((z < DEPTH - 1) & (source_z <= z))(lambda: up(source_z).wait_send())
        pl.when((z > 0) & (source_z >= z))(lambda: down(source_z).wait_send())


SPREAD_SEMS = [
    pltpu.SemaphoreType.DMA,
    pltpu.SemaphoreType.DMA((2, DEPTH)),
    pltpu.SemaphoreType.DMA((2, DEPTH)),
    pltpu.SemaphoreType.DMA((4, DEPTH)),
    pltpu.SemaphoreType.DMA((4, DEPTH)),
    pltpu.SemaphoreType.DMA((5, DEPTH)),
    pltpu.SemaphoreType.DMA((5, DEPTH)),
]


def gather_kernel(qkv_ref, proj_ref, expand_ref, contract_ref, misc_ref, out_ref, expand_bias, qv_bias, table,
                  own_ref, misc_out, misc_send, misc_recv, *sems):
    at = Place()
    start = 0
    for weight in (qkv_ref, proj_ref, expand_ref, contract_ref):
        own_ref[pl.ds(start, weight.shape[0])] = weight[...].astype(own_ref.dtype)
        start += weight.shape[0]
    at.greet()
    to_pair = remote(misc_ref, misc_out.at[at.mp_index], misc_send.at[0], misc_recv.at[0], at.partner)
    to_side = remote(misc_ref, misc_out.at[at.mp_index], misc_send.at[1], misc_recv.at[1], at.y_side)
    to_pair.start()
    to_side.start()
    misc_out[at.mp_index] = misc_ref[...]
    over = (1 - at.y) * 2 + at.core
    from_side = remote(misc_ref, misc_out.at[over], misc_send.at[1], misc_recv.at[1], at.y_side)
    relay = remote(misc_out.at[over], misc_out.at[over], misc_send.at[2], misc_recv.at[2], at.partner)
    spread(at, own_ref, out_ref, *sems)
    from_side.wait_recv()
    relay.start()
    beside = at.y * 2 + 1 - at.core
    remote(misc_ref, misc_out.at[beside], misc_send.at[0], misc_recv.at[0], at.partner).wait_recv()
    across = (1 - at.y) * 2 + 1 - at.core
    remote(misc_ref, misc_out.at[across], misc_send.at[2], misc_recv.at[2], at.partner).wait_recv()
    to_pair.wait_send()
    to_side.wait_send()
    relay.wait_send()
    for which in range(4):
        expand_bias[which] = misc_out[which, 0:1]
        for kind in range(2):
            qv_bias[kind : kind + 1, pl.ds(128 * which, 128)] = misc_out[which, 1:2, pl.ds(128 * kind, 128)]
        table[pl.ds(4 * which, 4)] = misc_out[which, 2:6, 0:256]


def gather_all(weights, misc):
    rows, columns = sum(weight.shape[0] for weight in weights), C
    vmem = pl.BlockSpec(memory_space=pltpu.VMEM)
    return pl.pallas_call(
        gather_kernel,
        out_shape=(
            jax.ShapeDtypeStruct((32, rows, columns), low),
            jax.ShapeDtypeStruct((4, 1, columns), wide),
            jax.ShapeDtypeStruct((2, columns), wide),
            jax.ShapeDtypeStruct((HEADS, 256), wide),
        ),
        in_specs=[vmem] * 5,
        out_specs=(pl.BlockSpec(memory_space=pl.ANY), vmem, vmem, vmem),
        scratch_shapes=[
            pltpu.VMEM((rows, columns), low),
            pltpu.VMEM((4,) + misc.shape, wide),
            pltpu.SemaphoreType.DMA((3,)),
            pltpu.SemaphoreType.DMA((3,)),
        ]
        + SPREAD_SEMS,
        compiler_params=pltpu.CompilerParams(collective_id=0, has_side_effects=True),
        name="gather_weights",
    )(*weights, misc)


def collect(at, grads, total_ref, mine, pair_buf, corner_x, corner_y, full_x, full_y, z_up, z_down, z_out,
            load_sem, pair_send, pair_recv, side_send, side_recv, z_send, z_recv):
    rows = total_ref.shape[0]
    half = rows // 2
    z, x, y, core = at.z, at.x, at.y, at.core
    low, high = pl.ds(0, half), pl.ds(half, rows - half)
    orders = ((3, 2, 1, 0), (3, 0, 2, 1), (0, 3, 1, 2), (0, 1, 2, 3))

    def turn(step):
        choice = jnp.int32(orders[3][step])
        for which in range(3):
            choice = jnp.where(z == which, jnp.int32(orders[which][step]), choice)
        return choice

    turns = [turn(step) for step in range(DEPTH)]

    def load(target, y_of):
        return pltpu.make_async_copy(
            grads.at[y_of * 2 + core, target], mine.at[y_of, target], load_sem.at[y_of, target]
        )

    def pair(target, y_of):
        return remote(
            grads.at[y_of * 2 + 1 - core, target], pair_buf.at[y_of, target],
            pair_send.at[y_of, target], pair_recv.at[y_of, target], at.partner,
        )

    def corner(kind, target):
        part = mine.at[1 - y, target, 1 - x]
        if kind == 0:
            return remote(part.at[low], corner_y.at[target], side_send.at[0, target], side_recv.at[0, target], at.y_side)
        return remote(part.at[high], corner_x.at[target], side_send.at[1, target], side_recv.at[1, target], at.x_side)

    def full(kind, target):
        if kind == 2:
            return remote(mine.at[y, target, 1 - x], full_x.at[target], side_send.at[2, target], side_recv.at[2, target], at.x_side)
        return remote(mine.at[1 - y, target, x], full_y.at[target], side_send.at[3, target], side_recv.at[3, target], at.y_side)

    def up(target):
        return remote(z_out.at[target], z_up.at[target], z_send.at[target], z_recv.at[0, target], at.above)

    def down(target):
        return remote(z_out.at[target], z_down.at[target], z_send.at[target], z_recv.at[1, target], at.below)

    wide = jnp.float32
    for target in turns:
        for y_of in (0, 1):
            pair(target, y_of).start()
            load(target, y_of).start()

    def first(target):
        for y_of in (0, 1):
            load(target, y_of).wait()
            pair(target, y_of).wait_recv()

        def add(which, carry):
            y_of, x_of = which // 2, which % 2
            mine[y_of, target, x_of] = (
                mine[y_of, target, x_of].astype(wide) + pair_buf[y_of, target, x_of].astype(wide)
            ).astype(mine.dtype)
            return carry

        lax.fori_loop(0, 4, add, 0)
        corner(0, target).start()
        corner(1, target).start()

    def second(target):
        corner(0, target).wait_recv()
        mine[y, target, 1 - x, low] = (
            mine[y, target, 1 - x, low].astype(wide) + corner_y[target].astype(wide)
        ).astype(mine.dtype)
        full(2, target).start()
        corner(1, target).wait_recv()
        mine[1 - y, target, x, high] = (
            mine[1 - y, target, x, high].astype(wide) + corner_x[target].astype(wide)
        ).astype(mine.dtype)
        full(3, target).start()

    def third(target, last):
        full(2, target).wait_recv()
        full(3, target).wait_recv()
        total_ref[...] = mine[y, target, x].astype(wide) + (
            full_x[target].astype(wide) + full_y[target].astype(wide)
        )

        def add_below():
            up(target).wait_recv()
            total_ref[...] += z_up[target].astype(wide)

        def add_above():
            down(target).wait_recv()
            total_ref[...] += z_down[target].astype(wide)

        pl.when((target >= z) & (z > 0))(add_below)
        pl.when((target <= z) & (z < DEPTH - 1))(add_above)
        if not last:
            z_out[target] = total_ref[...].astype(z_out.dtype)
            pl.when(target > z)(lambda: up(target).start())
            pl.when(target < z)(lambda: down(target).start())

    for step in range(DEPTH + 2):
        if step < DEPTH:
            first(turns[step])
        if 1 <= step <= DEPTH:
            second(turns[step - 1])
        if step >= 2:
            third(turns[step - 2], step - 2 == DEPTH - 1)
    for target in range(DEPTH):
        for y_of in (0, 1):
            pair(target, y_of).wait_send()
        for kind in (0, 1):
            corner(kind, target).wait_send()
        for kind in (2, 3):
            full(kind, target).wait_send()
        pl.when(target != z)(lambda: up(target).wait_send())


def collect_scratch(rows, columns, dtype):
    return [
        pltpu.VMEM((2, DEPTH, 2, rows, columns), dtype),
        pltpu.VMEM((2, DEPTH, 2, rows, columns), dtype),
        pltpu.VMEM((DEPTH, rows // 2, columns), dtype),
        pltpu.VMEM((DEPTH, rows // 2, columns), dtype),
        pltpu.VMEM((DEPTH, rows, columns), dtype),
        pltpu.VMEM((DEPTH, rows, columns), dtype),
        pltpu.VMEM((DEPTH, rows, columns), dtype),
        pltpu.VMEM((DEPTH, rows, columns), dtype),
        pltpu.VMEM((DEPTH, rows, columns), dtype),
        pltpu.SemaphoreType.DMA((2, DEPTH)),
        pltpu.SemaphoreType.DMA((2, DEPTH)),
        pltpu.SemaphoreType.DMA((2, DEPTH)),
        pltpu.SemaphoreType.DMA((4, DEPTH)),
        pltpu.SemaphoreType.DMA((4, DEPTH)),
        pltpu.SemaphoreType.DMA((DEPTH,)),
        pltpu.SemaphoreType.DMA((2, DEPTH)),
    ]


N_COLLECT = 16


def muon_kernel(grads, qkv_ref, proj_ref, expand_ref, contract_ref, grad_out, moment_out, next_all,
                own_next, *scratch):
    at = Place()
    at.greet()
    collect(at, grads, grad_out, *scratch[:N_COLLECT])
    start = 0
    for moment_ref in (qkv_ref, proj_ref, expand_ref, contract_ref):
        rows = pl.ds(start, moment_ref.shape[0])
        grad = grad_out[rows]
        moment = muon_beta * moment_ref[...] + grad
        moment_out[rows] = moment
        own_next[rows] = (grad + muon_beta * moment).astype(own_next.dtype)
        start += moment_ref.shape[0]
    spread(at, own_next, next_all, *scratch[N_COLLECT:])


def muon_exchange(grads, moments):
    rows, columns = sum(moment.shape[0] for moment in moments), C
    shape = jax.ShapeDtypeStruct((rows, columns), jnp.float32)
    vmem = pl.BlockSpec(memory_space=pltpu.VMEM)
    hbm = pl.BlockSpec(memory_space=pl.ANY)
    return pl.pallas_call(
        muon_kernel,
        out_shape=(shape, shape, jax.ShapeDtypeStruct((32, rows, columns), jnp.bfloat16)),
        in_specs=[hbm] + [vmem] * 4,
        out_specs=(vmem, vmem, hbm),
        scratch_shapes=[pltpu.VMEM((rows, columns), jnp.bfloat16)]
        + collect_scratch(rows, columns, jnp.bfloat16)
        + SPREAD_SEMS,
        compiler_params=pltpu.CompilerParams(
            collective_id=1, has_side_effects=True, vmem_limit_bytes=40 * 1024 * 1024
        ),
        name="muon_exchange",
    )(grads.reshape(4, DEPTH, 2, rows, columns), *moments)


def ns_kernel(next_all, own_images, small_ref, swapped, images_all, small_out,
              products, rows_buf, map_buf, small_parts, small_in, sem, keep_sem,
              act_send, act_recv, small_send, small_recv, swap_send, swap_recv):
    at = Place()
    mp_index, dp_index = at.mp_index, at.dp_index
    counts = (48, 16, 64, 64)
    pieces = own_images.shape[0]
    over = (1 - at.y) * 2 + at.core
    across = (1 - at.y) * 2 + 1 - at.core
    beside = at.y * 2 + 1 - at.core
    mp_peers = [{"dp": dp_index, "mp": lax.rem(mp_index + shift, 4)} for shift in (1, 2, 3)]
    small_peers = (at.y_side, at.partner, at.x_side, at.z_near, at.z_far)
    barrier = pltpu.get_barrier_semaphore()
    for device in (*mp_peers, at.x_side, at.z_near, at.z_far):
        pl.semaphore_signal(barrier, inc=1, device_id=device, device_id_type=MESH)

    def fetch(which):
        count = counts[which]
        copy = pltpu.make_async_copy(
            next_all.at[:, pl.ds(sum(counts[:which]), count)], rows_buf.at[:, pl.ds(0, count)], sem
        )
        copy.start()
        if count < 64:
            rows_buf[:, pl.ds(count, 64 - count)] = jnp.zeros((32, 64 - count, C), rows_buf.dtype)
        copy.wait()

    for which in range(4):
        pl.when(mp_index == which)(functools.partial(fetch, which))
    pl.semaphore_wait(barrier, 6)

    def slot(of_mp, image):
        return images_all.at[of_mp * pieces + image]

    def keep_copy(image):
        return pltpu.make_async_copy(own_images.at[image], slot(mp_index, image), keep_sem.at[image])

    def own_copy(which, image):
        device = (at.partner, at.y_side)[which]
        return remote(
            own_images.at[image], slot(mp_index, image), act_send.at[which, image], act_recv.at[which, image], device
        )

    def own_arrival(which, image):
        source, device = ((beside, at.partner), (over, at.y_side))[which]
        return remote(
            own_images.at[image], slot(source, image), act_send.at[which, image], act_recv.at[which, image], device
        )

    def relay(image):
        return remote(slot(over, image), slot(over, image), act_send.at[2, image], act_recv.at[2, image], at.partner)

    def relay_arrival(image):
        return remote(
            slot(across, image), slot(across, image), act_send.at[2, image], act_recv.at[2, image], at.partner
        )

    def small_copy(stage):
        source = small_ref if stage == 0 else small_parts.at[stage - 1]
        return remote(source, small_in.at[stage], small_send.at[stage], small_recv.at[stage], small_peers[stage])

    def small_step(stage):
        small_copy(stage).wait_recv()
        held = small_ref[...] if stage == 0 else small_parts[stage - 1]
        held = held + small_in[stage]
        if stage < 4:
            small_parts[stage] = held
            small_copy(stage + 1).start()
        else:
            small_out[...] = held

    small_copy(0).start()
    for image in range(pieces):
        own_copy(1, image).start()
    for image in range(pieces):
        own_copy(0, image).start()
        keep_copy(image).start()

    gram = None
    for part in range(4):
        block = rows_buf[8 * part : 8 * (part + 1)].reshape(512, C)
        term = dot_tn(block, block)
        gram = term if gram is None else gram + term
    eye = (
        lax.broadcasted_iota(jnp.int32, (C, C), 0) == lax.broadcasted_iota(jnp.int32, (C, C), 1)
    ).astype(wide)
    norm_value = jnp.sqrt(jnp.sum(jnp.sum(gram * eye, axis=1, keepdims=True), axis=0, keepdims=True)) + ns_eps
    gram = gram / (norm_value * norm_value)

    def dot_high(a, b):
        return jnp.dot(a, b, precision=lax.Precision.HIGH, preferred_element_type=wide)

    def pass_on(image):
        own_arrival(1, image).wait_recv()
        relay(image).start()

    total = None
    for iteration in range(NS_ITERS):
        square = dot_high(gram, gram)
        poly = coef_a * eye + (coef_b * gram + coef_c * square)
        total = poly if total is None else dot_high(total, poly)
        if iteration + 1 < NS_ITERS:
            gram = dot_high(dot_high(gram, poly), poly)
        pl.when(at.z >= 0)(functools.partial(small_step, iteration))
    map_buf[...] = total / norm_value

    def swap_copy(which):
        return remote(
            products.at[lax.rem(mp_index + which + 1, 4)], swapped.at[mp_index],
            swap_send.at[which], swap_recv.at[which], mp_peers[which],
        )

    for group in range(4):
        rows = rows_buf[group * 8 + dp_index].astype(wide)
        products[group] = dot_high(rows, map_buf[...]).astype(products.dtype)
    for which in (1, 2, 0):
        swap_copy(which).start()
    swapped[mp_index] = products[mp_index]
    for image in range(pieces):
        pass_on(image)
    for image in range(pieces):
        own_arrival(0, image).wait_recv()
        relay_arrival(image).wait_recv()
        own_copy(0, image).wait_send()
        own_copy(1, image).wait_send()
        relay(image).wait_send()
        keep_copy(image).wait()
    for which in range(3):
        source = lax.rem(mp_index + 3 - which, 4)
        remote(
            products.at[source], swapped.at[source], swap_send.at[which], swap_recv.at[which],
            {"dp": dp_index, "mp": source},
        ).wait_recv()
        swap_copy(which).wait_send()
    for stage in range(5):
        small_copy(stage).wait_send()


def newton_schulz_rows(next_all, own_images, small):
    vmem = pl.BlockSpec(memory_space=pltpu.VMEM)
    hbm = pl.BlockSpec(memory_space=pl.ANY)
    pieces = own_images.shape[0]
    return pl.pallas_call(
        ns_kernel,
        out_shape=(
            jax.ShapeDtypeStruct((4, 64, C), low),
            jax.ShapeDtypeStruct((4 * pieces,) + own_images.shape[1:], low),
            jax.ShapeDtypeStruct(small.shape, wide),
        ),
        in_specs=[hbm, vmem, vmem],
        out_specs=(vmem, hbm, vmem),
        scratch_shapes=[
            pltpu.VMEM((4, 64, C), low),
            pltpu.VMEM((32, 64, C), low),
            pltpu.VMEM((C, C), wide),
            pltpu.VMEM((4,) + small.shape, wide),
            pltpu.VMEM((5,) + small.shape, wide),
            pltpu.SemaphoreType.DMA,
            pltpu.SemaphoreType.DMA((pieces,)),
            pltpu.SemaphoreType.DMA((3, pieces)),
            pltpu.SemaphoreType.DMA((3, pieces)),
            pltpu.SemaphoreType.DMA((5,)),
            pltpu.SemaphoreType.DMA((5,)),
            pltpu.SemaphoreType.DMA((3,)),
            pltpu.SemaphoreType.DMA((3,)),
        ],
        compiler_params=pltpu.CompilerParams(
            collective_id=2, has_side_effects=True, vmem_limit_bytes=40 * 1024 * 1024
        ),
        name="newton_schulz",
    )(next_all, own_images, small)


def update_kernel(grads, moments, swapped, *refs):
    weights, outs = refs[:4], refs[4:]
    factors = (math.sqrt(3.0), 1.0, math.sqrt(max(1.0, FF / C)), 1.0)
    start = 0
    for which in range(4):
        count = weights[which].shape[0]
        rows = pl.ds(start, count)
        outs[which][...] = grads[rows]
        outs[4 + which][...] = moments[rows]
        part = swapped[which, pl.ds(0, count)].astype(wide)
        outs[8 + which][...] = -muon_rate * (muon_decay * weights[which][...] + factors[which] * part)
        start += count


def update_shards(grads, moments, swapped, weights):
    vmem = pl.BlockSpec(memory_space=pltpu.VMEM)
    shapes = [jax.ShapeDtypeStruct(weight.shape, wide) for weight in weights] * 3
    return pl.pallas_call(
        update_kernel,
        out_shape=shapes,
        in_specs=[vmem] * 7,
        out_specs=[vmem] * 12,
        name="update_shards",
    )(grads, moments, swapped, *weights)


def split_low(values):
    high = lax.reduce_precision(values, exponent_bits=8, mantissa_bits=7)
    return high.astype(jnp.bfloat16), (values - high).astype(jnp.bfloat16)


def dot_three(left, right):
    left_high, left_rest = left
    right_high, right_rest = right
    wide = dict(preferred_element_type=jnp.float32)
    return (
        jnp.dot(left_rest, right_high, **wide)
        + jnp.dot(left_high, right_rest, **wide)
        + jnp.dot(left_high, right_high, **wide)
    )


def newton_schulz(gram):
    width = gram.shape[0]
    eye = jnp.eye(width, dtype=jnp.float32)
    norm_value = jnp.sqrt(jnp.sum(gram * eye)) + ns_eps
    gram = gram / (norm_value * norm_value)
    total = None
    for iteration in range(NS_ITERS):
        parts = split_low(gram)
        square = dot_three(parts, parts)
        poly = coef_a * eye + (coef_b * gram + coef_c * square)
        poly_parts = split_low(poly)
        total = poly if total is None else dot_three(split_low(total), poly_parts)
        if iteration + 1 < NS_ITERS:
            half = dot_three(parts, poly_parts)
            gram = dot_three(split_low(half), poly_parts)
    return total / norm_value


def adam_update(grad_sum, first_moment, second_moment):
    first_new = adam_one * first_moment + (1.0 - adam_one) * grad_sum
    second_new = adam_two * second_moment + (1.0 - adam_two) * grad_sum * grad_sum
    first_hat = first_new / (1.0 - adam_one**adam_step)
    second_hat = second_new / (1.0 - adam_two**adam_step)
    return (-adam_rate * first_hat / (jnp.sqrt(second_hat) + adam_eps), first_new, second_new)


def exchange_plain(own_low, own_moments, rows):
    everyone = ("mp", "dp")
    starts = [sum(rows[:which]) for which in range(4)]

    def cut(stacked):
        return [stacked[:, start : start + count] for start, count in zip(starts, rows)]

    gathered = [
        part.reshape(-1, C) for part in cut(lax.all_gather(own_low, everyone, axis=0, tiled=False))
    ]

    def finish(big_local):
        mp_size, dp_size = lax.axis_size("mp"), lax.axis_size("dp")
        mp_index, dp_index = lax.axis_index("mp"), lax.axis_index("dp")
        devices = mp_size * dp_size
        stacked_grads = jnp.concatenate(
            [grad.reshape(devices, count, C) for grad, count in zip(big_local, rows)], axis=1
        )
        own_grads = lax.psum_scatter(
            stacked_grads.reshape(devices * sum(rows), C), everyone, scatter_dimension=0, tiled=True
        ).astype(wide)
        own_buffers = muon_beta * own_moments + own_grads
        own_nesterov = own_grads + muon_beta * own_buffers
        iterate_all = lax.all_gather(own_nesterov.astype(low), everyone, axis=0, tiled=False)
        grams = jnp.stack([dot_tn(part.reshape(-1, C), part.reshape(-1, C)) for part in cut(iterate_all)])
        ortho_map = newton_schulz(lax.dynamic_index_in_dim(grams, mp_index, 0, keepdims=False))
        most = max(rows)
        picked = lax.dynamic_slice(
            iterate_all.reshape(mp_size, dp_size, sum(rows), C),
            (
                jnp.int32(0),
                dp_index.astype(jnp.int32),
                jnp.array(starts, jnp.int32)[mp_index],
                jnp.int32(0),
            ),
            (mp_size, 1, most, C),
        ).reshape(mp_size * most, C)
        map_parts = split_low(ortho_map)
        products = dot(picked, map_parts[0]) + dot(picked, map_parts[1])
        swapped = lax.all_to_all(products.reshape(mp_size, most, C), "mp", 0, 0, tiled=False)
        return own_grads, own_buffers, swapped

    return gathered, finish


def shards(
    images,
    cotangent,
    qkv_weight,
    proj_weight,
    expand_weight,
    contract_weight,
    qkv_moment,
    proj_moment,
    expand_moment,
    contract_moment,
    vectors,
    qv_bias,
    expand_bias,
    rel_table,
    vectors_first,
    vectors_second,
    qv_first,
    qv_second,
    expand_bias_first,
    expand_bias_second,
    table_first,
    table_second,
    region_ids,
    pos_index,
    image_counts,
):
    everyone = ("mp", "dp")
    mp_size, dp_size = lax.axis_size("mp"), lax.axis_size("dp")
    mp_index = lax.axis_index("mp")
    linked = mp_size == 4 and dp_size == 8
    per_device = IMG_DEV // mp_size
    first_image = (mp_index * per_device).astype(jnp.int32)
    place = jnp.stack([first_image, image_counts[0]])
    own_images = lax.dynamic_slice_in_dim(images, first_image, per_device, 0)
    own_cotangent = lax.dynamic_slice_in_dim(cotangent, first_image, per_device, 0)
    weights_all = (qkv_weight, proj_weight, expand_weight, contract_weight)
    rows = [weight.shape[0] for weight in weights_all]
    starts = [sum(rows[:which]) for which in range(4)]
    moments = (qkv_moment, proj_moment, expand_moment, contract_moment)
    if linked:
        misc = jnp.concatenate(
            [
                expand_bias[None],
                jnp.pad(qv_bias.reshape(1, -1), ((0, 0), (0, C - qv_bias.size))),
                jnp.pad(rel_table.T, ((0, 2), (0, C - TABLE))),
            ],
            axis=0,
        )
        gathered, expand_full, qv_full, table_wide = gather_all(weights_all, misc)
        table_full = table_wide[:, :TABLE]
    else:
        own_low = jnp.concatenate([weight.astype(low) for weight in weights_all], axis=0)
        own_moments = jnp.concatenate(moments, axis=0)
        gathered, finish_plain = exchange_plain(own_low, own_moments, rows)
        qv_full = lax.all_gather(qv_bias, "mp", axis=1, tiled=True)
        expand_full = lax.all_gather(expand_bias, "mp", axis=0, tiled=True).reshape(4, C)
        table_full = lax.all_gather(rel_table.T, "mp", axis=0, tiled=True)
    onehot = (
        jnp.arange(TABLE, dtype=jnp.int32)[:, None] == pos_index.reshape(1, SPAN * SPAN)
    ).astype(wide)
    pos_bias = jnp.dot(table_full, onehot, precision=highest).reshape(HEADS, SPAN, SPAN)
    window_regions = to_windows(region_ids.reshape(1, TOK, 1))[:, :, 0]
    window_mask = jnp.where(
        window_regions[:, :, None] != window_regions[:, None, :], mask_value, 0.0
    ).astype(wide)
    bias = pair_bias(pos_bias, window_mask)
    block_low, input_low, big_local, small_rows, table_pairs = run_layer(
        linked, per_device, place, own_images, own_cotangent, vectors, qv_full, expand_full, bias, gathered
    )
    if linked:
        block_out = block_low
    else:
        block_out = lax.all_gather(block_low, "mp", axis=0, tiled=True)
        input_grad = lax.all_gather(input_low, "mp", axis=0, tiled=True)
    pairs = table_pairs.reshape(HEADS, PAIR, PAIR)
    bias_heads = pairs[:, :SPAN, :SPAN] + pairs[:, SPAN : 2 * SPAN, SPAN : 2 * SPAN]
    table_local = lax.dot_general(
        bias_heads.reshape(HEADS, SPAN * SPAN),
        onehot,
        (((1,), (1,)), ((), ())),
        precision=highest,
        preferred_element_type=wide,
    )
    if linked:
        small_own = jnp.concatenate(
            [small_rows, jnp.pad(table_local, ((0, 0), (0, C - TABLE)))], axis=0
        )
        own_grads, own_buffers, next_all = muon_exchange(big_local, moments)
        swapped, input_grad, small_all = newton_schulz_rows(next_all, input_low, small_own)
        small_full, table_all = small_all[:HEADS], small_all[HEADS:, :TABLE]
    else:
        small_full, table_all = lax.psum((small_rows, table_local), everyone)
        own_grads, own_buffers, swapped = finish_plain(big_local)
    updated = update_shards(own_grads, own_buffers, swapped, weights_all)
    shares, buffers, new_steps = updated[:4], updated[4:8], updated[8:]

    def own_columns(full, width):
        return lax.dynamic_slice_in_dim(full, mp_index * width, width, full.ndim - 1)

    small_sums = (
        small_full[:6],
        own_columns(small_full[6:8], qv_bias.shape[1]),
        own_columns(small_full[8:12].reshape(FF), expand_bias.shape[0]),
        lax.dynamic_slice_in_dim(table_all, mp_index * rel_table.shape[1], rel_table.shape[1], 0).T,
    )
    vectors_step, vectors_first_new, vectors_second_new = adam_update(
        small_sums[0], vectors_first, vectors_second
    )
    qv_step, qv_first_new, qv_second_new = adam_update(small_sums[1], qv_first, qv_second)
    expand_bias_step, expand_bias_first_new, expand_bias_second_new = adam_update(
        small_sums[2], expand_bias_first, expand_bias_second
    )
    table_step, table_first_new, table_second_new = adam_update(
        small_sums[3], table_first, table_second
    )
    return (
        block_out,
        input_grad,
        shares[0],
        shares[1],
        shares[2],
        shares[3],
        small_sums[0],
        small_sums[1],
        small_sums[2],
        small_sums[3],
        new_steps[0],
        new_steps[1],
        new_steps[2],
        new_steps[3],
        buffers[0],
        buffers[1],
        buffers[2],
        buffers[3],
        vectors_step,
        qv_step,
        expand_bias_step,
        table_step,
        vectors_first_new,
        vectors_second_new,
        qv_first_new,
        qv_second_new,
        expand_bias_first_new,
        expand_bias_second_new,
        table_first_new,
        table_second_new,
    )


def solution(mesh):
    return jax.shard_map(
        shards,
        mesh=mesh,
        in_specs=(
            P("dp", None, None),
            P("dp", None, None),
            P(("mp", "dp"), None),
            P(("mp", "dp"), None),
            P(("mp", "dp"), None),
            P(("mp", "dp"), None),
            P(("mp", "dp"), None),
            P(("mp", "dp"), None),
            P(("mp", "dp"), None),
            P(("mp", "dp"), None),
            P(),
            P(None, "mp"),
            P("mp"),
            P(None, "mp"),
            P(),
            P(),
            P(None, "mp"),
            P(None, "mp"),
            P("mp"),
            P("mp"),
            P(None, "mp"),
            P(None, "mp"),
            P(),
            P(),
            P("dp"),
        ),
        out_specs=(
            P("dp", None, None),
            P("dp", None, None),
            P(("mp", "dp"), None),
            P(("mp", "dp"), None),
            P(("mp", "dp"), None),
            P(("mp", "dp"), None),
            P(),
            P(None, "mp"),
            P("mp"),
            P(None, "mp"),
            P(("mp", "dp"), None),
            P(("mp", "dp"), None),
            P(("mp", "dp"), None),
            P(("mp", "dp"), None),
            P(("mp", "dp"), None),
            P(("mp", "dp"), None),
            P(("mp", "dp"), None),
            P(("mp", "dp"), None),
            P(),
            P(None, "mp"),
            P("mp"),
            P(None, "mp"),
            P(),
            P(),
            P(None, "mp"),
            P(None, "mp"),
            P("mp"),
            P("mp"),
            P(None, "mp"),
            P(None, "mp"),
        ),
        check_vma=False,
    )
```

profile of v0, /device:TPU:1, one launch (start us, length us, event | category | flops | bytes accessed | tf_op | source)
XLA Modules:
  0.0 234.0 jit_solution(2752800346339278161)
XLA Ops:
  0.7 0.7 slice.60
  1.4 0.7 slice.61
  2.1 0.1 slice_add_fusion.1
  2.1 0.1 pad_add_fusion.1
  2.2 0.1 reshape.93
  2.3 0.1 reshape.98
  2.4 0.1 compare_select_fusion
  2.5 1.3 select_maximum_fusion.2.misc_ref
  3.8 38.3 %gather_weights.1 = (bf16[32,192,512]{2,1,0:T(8,128)(2,1)}, f32[4,1,512]{2,1,0:T(1,128)}, f32[2,512]{1,0:T(2,128)}, f32[16,256]{1,0:T(8,128)}) custom-call(f32[48,512]{1,0:T(8,128)} %refs_0_.1, f32[16,512]{1,0:T(8,128)} %refs_1_.1, f32[64,512]{1,0:T(8,128)} %refs_2_.1, f32[64,512]{1,0:T(8,128)} %refs_3_.1, f32[8,512]{1,0:T(8,128)} %select_maximum_fusion.2.misc_ref), custom_call_target="tpu_custom_call" | custom-call | tf_op jit(solution)/shard_map/gather_weights/pallas_call | solution.py:719
  42.1 0.9 eq.16
  43.0 1.4 fusion.3
  44.4 0.2 add.89
  44.6 0.1 broadcast_add_fusion
  44.7 0.1 slice_bitcast_fusion.1
  44.9 1.6 fusion
  46.4 2.7 %constant_dynamic-slice_fusion.1 = (bf16[4,196,512]{2,0,1:T(4,128)(2,1)S(1)}, bf16[4,196,512]{2,0,1:T(4,128)(2,1)S(1)}) fusion(bf16[16,196,512]{2,0,1:T(8,128)(2,1)} %param.28, s32[]{:T(128)S(6)} %select_n.23, bf16[16,196,512]{2,0,1:T(8,128)(2,1)} %param.27), kind=kLoop, calls=%fused_computation.48 | loop fusion | bytes 3211268 | tf_op jit(solution)/shard_map/dynamic_slice | solution.py:1238
  49.2 1.0 copy.70.images
  50.2 1.1 copy.71.cotangent
  51.9 0.6 pad_add_fusion.2.place
  52.5 67.3 %window_layer.1 = (bf16[16,196,512]{2,1,0:T(8,128)(2,1)}, bf16[4,196,512]{2,1,0:T(8,128)(2,1)}, bf16[16,2,192,512]{3,2,1,0:T(8,128)(2,1)}, f32[16,512]{1,0:T(8,128)}, f32[4,448,112]{2,1,0:T(8,128)}) custom-call(s32[2]{0:T(128)} %pad_add_fusion.2.place, bf16[4,196,512]{2,1,0:T(8,128)(2,1)} %copy.70.images, bf16[4,196,512]{2,1,0:T(8,128)(2,1)} %copy.71.cotangent, ...), custom_call_target="tpu_custom_call" | custom-call | tf_op jit(solution)/shard_map/window_layer/pallas_call | solution.py:430
  119.8 0.0 copy-start.9
  119.8 0.0 copy-start.5
  119.8 0.0 copy-start.6
  119.8 0.0 copy-start.7
  119.8 0.0 copy-start.8
  119.9 1.4 slice_add_fusion
  121.3 0.2 reshape.96
  121.5 0.9 fusion.2
  122.4 0.0 copy-done.9
  122.4 0.0 copy-done.5
  122.4 0.0 copy-done.6
  122.4 0.0 copy-done.7
  122.4 0.0 copy-done.8
  122.5 0.0 copy-start
  122.5 2.8 %copy-done = bf16[16,2,192,512]{3,2,1,0:T(8,128)(2,1)S(1)} copy-done((bf16[16,2,192,512]{3,2,1,0:T(8,128)(2,1)S(1)}, bf16[16,2,192,512]{3,2,1,0:T(8,128)(2,1)}, u32[]{:S(2)}) %copy-start) | copy-done | bytes 6291480
  125.2 66.1 %muon_exchange.1 = (f32[192,512]{1,0:T(8,128)S(1)}, f32[192,512]{1,0:T(8,128)S(1)}, bf16[32,192,512]{2,1,0:T(8,128)(2,1)S(1)}) custom-call(bf16[4,4,2,192,512]{4,3,2,1,0:T(8,128)(2,1)S(1)} %bitcast.24, f32[48,512]{1,0:T(8,128)S(1)} %copy-done.7, f32[16,512]{1,0:T(8,128)S(1)} %copy-done.8, f32[64,512]{1,0:T(8,128)S(1)} %copy-done.5, f32[64,512]{1,0:T(8,128)S(1)} %copy-done.6), custom_call_target="tpu_custom_call" | custom-call | tf_op jit(solution)/shard_map/muon_exchange/pallas_call | solution.py:903
  191.4 0.0 copy-start.3
  191.4 0.7 copy-done.3
  192.1 0.0 copy-done.1
  192.1 28.2 %newton_schulz.1 = (bf16[4,64,512]{2,1,0:T(8,128)(2,1)S(1)}, bf16[16,196,512]{2,1,0:T(8,128)(2,1)S(1)}, f32[32,512]{1,0:T(8,128)S(1)}) custom-call(bf16[32,192,512]{2,1,0:T(8,128)(2,1)S(1)} %get-tuple-element.63.next_all, bf16[4,196,512]{2,1,0:T(8,128)(2,1)S(1)} %copy-done.1, f32[32,512]{1,0:T(8,128)S(1)} %select_maximum_fusion.1.small_ref), custom_call_target="tpu_custom_call" | custom-call | tf_op jit(solution)/shard_map/newton_schulz/pallas_call | solution.py:1059
  220.4 0.0 copy-done.2
  220.4 0.0 copy-start.4
  220.4 0.7 copy-done.4
  221.1 2.4 %update_shards.1 = (f32[48,512]{1,0:T(8,128)}, f32[16,512]{1,0:T(8,128)}, f32[64,512]{1,0:T(8,128)}, f32[64,512]{1,0:T(8,128)}, f32[48,512]{1,0:T(8,128)}, /*ind...) custom-call(f32[192,512]{1,0:T(8,128)} %copy-done.2, ...), custom_call_target="tpu_custom_call" | custom-call | tf_op jit(solution)/shard_map/update_shards/pallas_call | solution.py:1107
  223.5 0.0 copy-start.12
  223.5 0.0 copy-start.13
  223.5 0.0 copy-start.14
  223.5 0.0 copy-start.15
  223.5 0.0 copy-start.16
  223.5 0.0 copy-start.17
  223.5 2.8 %copy.67 = bf16[16,196,512]{2,0,1:T(8,128)(2,1)} copy(bf16[16,196,512]{2,1,0:T(8,128)(2,1)S(1)} %get-tuple-element.115) | data formatting | bytes 6422528
  226.3 0.0 copy-done.10
  226.3 0.0 copy-done.11
  226.3 0.6 add_divide_fusion
  226.9 0.0 copy-done.12
  226.9 0.0 copy-done.13
  226.9 0.6 add_divide_fusion.1
  227.6 0.0 copy-done.14
  227.6 0.0 copy-done.15
  227.6 0.7 add_divide_fusion.2
  228.3 0.0 copy-done.16
  228.3 0.0 copy-done.17
  228.3 0.6 add_divide_fusion.3
  228.9 4.7 %copy.66 = bf16[16,196,512]{2,0,1:T(8,128)(2,1)} copy(bf16[16,196,512]{2,1,0:T(8,128)(2,1)} %get-tuple-element.114) | data formatting | bytes 6422528
  (13 shorter events, 0.1 us)
Async XLA Ops:
  119.8 2.6 %copy-start.9 = (f32[16,512]{1,0:T(8,128)S(1)}, f32[16,512]{1,0:T(8,128)}, u32[]{:S(2)}) copy-start(f32[16,512]{1,0:T(8,128)} %get-tuple-element.65) | copy-start | bytes 98308
  119.8 2.6 %copy-start.5 = (f32[64,512]{1,0:T(8,128)S(1)}, f32[64,512]{1,0:T(8,128)}, u32[]{:S(2)}) copy-start(f32[64,512]{1,0:T(8,128)} %expand_ref.3) | copy-start | bytes 393220
  119.8 2.6 %copy-start.6 = (f32[64,512]{1,0:T(8,128)S(1)}, f32[64,512]{1,0:T(8,128)}, u32[]{:S(2)}) copy-start(f32[64,512]{1,0:T(8,128)} %contract_ref.3) | copy-start | bytes 393220
  119.8 2.6 %copy-start.7 = (f32[48,512]{1,0:T(8,128)S(1)}, f32[48,512]{1,0:T(8,128)}, u32[]{:S(2)}) copy-start(f32[48,512]{1,0:T(8,128)} %qkv_ref.3) | copy-start | bytes 294916
  119.8 2.6 %copy-start.8 = (f32[16,512]{1,0:T(8,128)S(1)}, f32[16,512]{1,0:T(8,128)}, u32[]{:S(2)}) copy-start(f32[16,512]{1,0:T(8,128)} %proj_ref.3) | copy-start | bytes 98308
  122.5 2.8 %copy-start = (bf16[16,2,192,512]{3,2,1,0:T(8,128)(2,1)S(1)}, bf16[16,2,192,512]{3,2,1,0:T(8,128)(2,1)}, u32[]{:S(2)}) copy-start(bf16[16,2,192,512]{3,2,1,0:T(8,128)(2,1)} %get-tuple-element.62) | copy-start | bytes 18874372
  125.2 66.9 %copy-start.1 = (bf16[4,196,512]{2,1,0:T(8,128)(2,1)S(1)}, bf16[4,196,512]{2,1,0:T(8,128)(2,1)}, u32[]{:S(2)}) copy-start(bf16[4,196,512]{2,1,0:T(8,128)(2,1)} %get-tuple-element.64.own_images) | copy-start | bytes 2408452
  191.4 0.7 copy-start.3
  192.1 28.2 %copy-start.2 = (f32[192,512]{1,0:T(8,128)}, f32[192,512]{1,0:T(8,128)S(1)}, u32[]{:S(2)}) copy-start(f32[192,512]{1,0:T(8,128)S(1)} %get-tuple-element.68.grads) | copy-start | bytes 1179652
  220.4 0.7 copy-start.4
  223.4 2.8 %copy-start.10 = (f32[6,512]{1,0:T(8,128)S(1)}, f32[6,512]{1,0:T(8,128)}, u32[]{:S(2)}) copy-start(f32[6,512]{1,0:T(8,128)} %param.41) | copy-start | bytes 36868
  223.4 2.8 %copy-start.11 = (f32[6,512]{1,0:T(8,128)S(1)}, f32[6,512]{1,0:T(8,128)}, u32[]{:S(2)}) copy-start(f32[6,512]{1,0:T(8,128)} %param.42) | copy-start | bytes 36868
  223.5 3.5 %copy-start.12 = (f32[169,4]{0,1:T(4,128)S(1)}, f32[169,4]{0,1:T(4,128)}, u32[]{:S(2)}) copy-start(f32[169,4]{0,1:T(4,128)} %param.47) | copy-start | bytes 8116
  223.5 3.5 %copy-start.13 = (f32[169,4]{0,1:T(4,128)S(1)}, f32[169,4]{0,1:T(4,128)}, u32[]{:S(2)}) copy-start(f32[169,4]{0,1:T(4,128)} %param.48) | copy-start | bytes 8116
  223.5 4.1 %copy-start.14 = (f32[512]{0:T(512)S(1)}, f32[512]{0:T(512)}, u32[]{:S(2)}) copy-start(f32[512]{0:T(512)} %param.45) | copy-start | bytes 6148
  223.5 4.1 %copy-start.15 = (f32[512]{0:T(512)S(1)}, f32[512]{0:T(512)}, u32[]{:S(2)}) copy-start(f32[512]{0:T(512)} %param.46) | copy-start | bytes 6148
  223.5 4.8 %copy-start.16 = (f32[2,128]{1,0:T(2,128)S(1)}, f32[2,128]{1,0:T(2,128)}, u32[]{:S(2)}) copy-start(f32[2,128]{1,0:T(2,128)} %param.43) | copy-start | bytes 3076
  223.5 4.8 %copy-start.17 = (f32[2,128]{1,0:T(2,128)S(1)}, f32[2,128]{1,0:T(2,128)}, u32[]{:S(2)}) copy-start(f32[2,128]{1,0:T(2,128)} %param.44) | copy-start | bytes 3076
where the time goes:
time: 238 us; the launch traced here: 234 us
  Pallas kernels  202 us (85%)
  local copies, waits for them, and re-layouts  19.5 us (8%)
  other arithmetic  7.85 us (3%)
    pallas_call x1, Pallas kernels, run_layer(): pl.pallas_call(functools.partial(layer_kernel, packed, batch), out_shape=...  67.3 us
    pallas_call x1, Pallas kernels, muon_exchange(): pl.pallas_call(muon_kernel, out_shape=(shape, shape, jax.ShapeDtypeStruct...  66.1 us
    pallas_call x1, Pallas kernels, gather_all(): pl.pallas_call(gather_kernel, out_shape=(jax.ShapeDtypeStruct((32, rows,...  38.3 us
    pallas_call x1, Pallas kernels, newton_schulz_rows(): pl.pallas_call(ns_kernel, out_shape=(jax.ShapeDtypeStruct((4, 64, C), low...  28.2 us
    unnamed x42, local copies, waits for them, and re-layouts  13.9 us

commit v1 on v0

--- a/solution.py
+++ b/solution.py
@@ -916,7 +916,7 @@
 
 
 def ns_kernel(next_all, own_images, small_ref, swapped, images_all, small_out,
-              products, rows_buf, map_buf, small_parts, small_in, sem, keep_sem,
+              products, rows_buf, map_buf, gram_buf, total_buf, small_parts, small_in, sem, keep_sem,
               act_send, act_recv, small_send, small_recv, swap_send, swap_recv):
     at = Place()
     mp_index, dp_index = at.mp_index, at.dp_index
@@ -941,8 +941,6 @@
             rows_buf[:, pl.ds(count, 64 - count)] = jnp.zeros((32, 64 - count, C), rows_buf.dtype)
         copy.wait()
 
-    for which in range(4):
-        pl.when(mp_index == which)(functools.partial(fetch, which))
     pl.semaphore_wait(barrier, 6)
 
     def slot(of_mp, image):
@@ -991,6 +989,9 @@
     for image in range(pieces):
         own_copy(0, image).start()
         keep_copy(image).start()
+
+    for which in range(4):
+        pl.when(mp_index == which)(functools.partial(fetch, which))
 
     gram = None
     for part in range(4):
@@ -1010,14 +1011,28 @@
         own_arrival(1, image).wait_recv()
         relay(image).start()
 
-    total = None
-    for iteration in range(NS_ITERS):
+    def poly_of(gram):
         square = dot_high(gram, gram)
-        poly = coef_a * eye + (coef_b * gram + coef_c * square)
-        total = poly if total is None else dot_high(total, poly)
-        if iteration + 1 < NS_ITERS:
-            gram = dot_high(dot_high(gram, poly), poly)
-        pl.when(at.z >= 0)(functools.partial(small_step, iteration))
+        return coef_a * eye + (coef_b * gram + coef_c * square)
+
+    gram_buf[...] = gram
+    poly = poly_of(gram)
+    total_buf[...] = poly
+    gram_buf[...] = dot_high(dot_high(gram, poly), poly)
+    pl.when(at.z >= 0)(functools.partial(small_step, 0))
+
+    def iterate(iteration, carry):
+        gram = gram_buf[...]
+        poly = poly_of(gram)
+        total_buf[...] = dot_high(total_buf[...], poly)
+        gram_buf[...] = dot_high(dot_high(gram, poly), poly)
+        for which in range(1, NS_ITERS - 1):
+            pl.when(iteration == which)(functools.partial(small_step, which))
+        return carry
+
+    lax.fori_loop(1, NS_ITERS - 1, iterate, 0)
+    total = dot_high(total_buf[...], poly_of(gram_buf[...]))
+    pl.when(at.z >= 0)(functools.partial(small_step, NS_ITERS - 1))
     map_buf[...] = total / norm_value
 
     def swap_copy(which):
@@ -1068,6 +1083,8 @@
         scratch_shapes=[
             pltpu.VMEM((4, 64, C), low),
             pltpu.VMEM((32, 64, C), low),
+            pltpu.VMEM((C, C), wide),
+            pltpu.VMEM((C, C), wide),
             pltpu.VMEM((C, C), wide),
             pltpu.VMEM((4,) + small.shape, wide),
             pltpu.VMEM((5,) + small.shape, wide),

time: 238 us -> 234 us (0.983); the launches traced: 234 us -> 234 us
  no operation moved by 1% of the time
where the time goes in v1:
time: 234 us
  Pallas kernels  202 us (86%)
  local copies, waits for them, and re-layouts  19.5 us (8%)
  other arithmetic  7.85 us (3%)
    pallas_call x1, Pallas kernels, run_layer(): pl.pallas_call(functools.partial(layer_kernel, packed, batch), out_shape=...  67.3 us
    pallas_call x1, Pallas kernels, muon_exchange(): pl.pallas_call(muon_kernel, out_shape=(shape, shape, jax.ShapeDtypeStruct...  66.1 us
    pallas_call x1, Pallas kernels, gather_all(): pl.pallas_call(gather_kernel, out_shape=(jax.ShapeDtypeStruct((32, rows,...  38.3 us
    pallas_call x1, Pallas kernels, newton_schulz_rows(): pl.pallas_call(ns_kernel, out_shape=(jax.ShapeDtypeStruct((4, 64, C), low...  28.4 us
    unnamed x42, local copies, waits for them, and re-layouts  13.9 us

profile of v1, /device:TPU:1, one launch (start us, length us, event | category | flops | bytes accessed | tf_op | source)
XLA Modules:
  0.0 233.7 jit_solution(5127755426623617673)
XLA Ops:
  0.7 0.7 slice.60
  1.4 0.7 slice.61
  2.1 0.1 slice_add_fusion.1
  2.1 0.1 pad_add_fusion.1
  2.2 0.1 reshape.93
  2.3 0.1 reshape.98
  2.4 0.1 compare_select_fusion
  2.5 1.3 select_maximum_fusion.2.misc_ref
  3.8 38.3 %gather_weights.1 = (bf16[32,192,512]{2,1,0:T(8,128)(2,1)}, f32[4,1,512]{2,1,0:T(1,128)}, f32[2,512]{1,0:T(2,128)}, f32[16,256]{1,0:T(8,128)}) custom-call(f32[48,512]{1,0:T(8,128)} %refs_0_.1, f32[16,512]{1,0:T(8,128)} %refs_1_.1, f32[64,512]{1,0:T(8,128)} %refs_2_.1, f32[64,512]{1,0:T(8,128)} %refs_3_.1, f32[8,512]{1,0:T(8,128)} %select_maximum_fusion.2.misc_ref), custom_call_target="tpu_custom_call" | custom-call | tf_op jit(solution)/shard_map/gather_weights/pallas_call | solution.py:719
  42.1 0.9 eq.16
  43.0 1.4 fusion.3
  44.4 0.2 add.89
  44.6 0.1 broadcast_add_fusion
  44.7 0.1 slice_bitcast_fusion.1
  44.9 1.6 fusion
  46.4 2.7 %constant_dynamic-slice_fusion.1 = (bf16[4,196,512]{2,0,1:T(4,128)(2,1)S(1)}, bf16[4,196,512]{2,0,1:T(4,128)(2,1)S(1)}) fusion(bf16[16,196,512]{2,0,1:T(8,128)(2,1)} %param.28, s32[]{:T(128)S(6)} %select_n.23, bf16[16,196,512]{2,0,1:T(8,128)(2,1)} %param.27), kind=kLoop, calls=%fused_computation.48 | loop fusion | bytes 3211268 | tf_op jit(solution)/shard_map/dynamic_slice | solution.py:1255
  49.2 1.0 copy.70.images
  50.2 1.1 copy.71.cotangent
  51.9 0.6 pad_add_fusion.2.place
  52.5 67.3 %window_layer.1 = (bf16[16,196,512]{2,1,0:T(8,128)(2,1)}, bf16[4,196,512]{2,1,0:T(8,128)(2,1)}, bf16[16,2,192,512]{3,2,1,0:T(8,128)(2,1)}, f32[16,512]{1,0:T(8,128)}, f32[4,448,112]{2,1,0:T(8,128)}) custom-call(s32[2]{0:T(128)} %pad_add_fusion.2.place, bf16[4,196,512]{2,1,0:T(8,128)(2,1)} %copy.70.images, bf16[4,196,512]{2,1,0:T(8,128)(2,1)} %copy.71.cotangent, ...), custom_call_target="tpu_custom_call" | custom-call | tf_op jit(solution)/shard_map/window_layer/pallas_call | solution.py:430
  119.8 0.0 copy-start.9
  119.8 0.0 copy-start.5
  119.8 0.0 copy-start.6
  119.8 0.0 copy-start.7
  119.8 0.0 copy-start.8
  119.9 1.4 slice_add_fusion
  121.3 0.2 reshape.96
  121.5 0.9 fusion.2
  122.4 0.0 copy-done.9
  122.4 0.0 copy-done.5
  122.4 0.0 copy-done.6
  122.4 0.0 copy-done.7
  122.5 0.0 copy-done.8
  122.5 0.0 copy-start
  122.5 2.8 %copy-done = bf16[16,2,192,512]{3,2,1,0:T(8,128)(2,1)S(1)} copy-done((bf16[16,2,192,512]{3,2,1,0:T(8,128)(2,1)S(1)}, bf16[16,2,192,512]{3,2,1,0:T(8,128)(2,1)}, u32[]{:S(2)}) %copy-start) | copy-done | bytes 6291480
  125.2 66.1 %muon_exchange.1 = (f32[192,512]{1,0:T(8,128)S(1)}, f32[192,512]{1,0:T(8,128)S(1)}, bf16[32,192,512]{2,1,0:T(8,128)(2,1)S(1)}) custom-call(bf16[4,4,2,192,512]{4,3,2,1,0:T(8,128)(2,1)S(1)} %bitcast.24, f32[48,512]{1,0:T(8,128)S(1)} %copy-done.7, f32[16,512]{1,0:T(8,128)S(1)} %copy-done.8, f32[64,512]{1,0:T(8,128)S(1)} %copy-done.5, f32[64,512]{1,0:T(8,128)S(1)} %copy-done.6), custom_call_target="tpu_custom_call" | custom-call | tf_op jit(solution)/shard_map/muon_exchange/pallas_call | solution.py:903
  191.4 0.0 copy-start.3
  191.4 0.7 copy-done.3
  192.2 0.0 copy-done.1
  192.2 28.4 %newton_schulz.1 = (bf16[4,64,512]{2,1,0:T(8,128)(2,1)S(1)}, bf16[16,196,512]{2,1,0:T(8,128)(2,1)S(1)}, f32[32,512]{1,0:T(8,128)S(1)}) custom-call(bf16[32,192,512]{2,1,0:T(8,128)(2,1)S(1)} %get-tuple-element.63.next_all, bf16[4,196,512]{2,1,0:T(8,128)(2,1)S(1)} %copy-done.1, f32[32,512]{1,0:T(8,128)S(1)} %select_maximum_fusion.1.small_ref), custom_call_target="tpu_custom_call" | custom-call | tf_op jit(solution)/shard_map/newton_schulz/pallas_call | solution.py:1074
  220.5 0.0 copy-done.2
  220.6 0.0 copy-start.4
  220.6 0.7 copy-done.4
  221.3 2.4 %update_shards.1 = (f32[48,512]{1,0:T(8,128)}, f32[16,512]{1,0:T(8,128)}, f32[64,512]{1,0:T(8,128)}, f32[64,512]{1,0:T(8,128)}, f32[48,512]{1,0:T(8,128)}, /*ind...) custom-call(f32[192,512]{1,0:T(8,128)} %copy-done.2, ...), custom_call_target="tpu_custom_call" | custom-call | tf_op jit(solution)/shard_map/update_shards/pallas_call | solution.py:1124
  223.6 0.0 copy-start.12
  223.7 0.0 copy-start.13
  223.7 0.0 copy-start.14
  223.7 0.0 copy-start.15
  223.7 0.0 copy-start.16
  223.7 0.0 copy-start.17
  223.7 2.8 %copy.67 = bf16[16,196,512]{2,0,1:T(8,128)(2,1)} copy(bf16[16,196,512]{2,1,0:T(8,128)(2,1)S(1)} %get-tuple-element.115) | data formatting | bytes 6422528
  226.5 0.0 copy-done.10
  226.5 0.0 copy-done.11
  226.5 0.6 add_divide_fusion
  227.1 0.0 copy-done.12
  227.1 0.0 copy-done.13
  227.1 0.6 add_divide_fusion.1
  227.8 0.0 copy-done.14
  227.8 0.0 copy-done.15
  227.8 0.7 add_divide_fusion.2
  228.5 0.0 copy-done.16
  228.5 0.0 copy-done.17
  228.5 0.6 add_divide_fusion.3
  229.1 4.7 %copy.66 = bf16[16,196,512]{2,0,1:T(8,128)(2,1)} copy(bf16[16,196,512]{2,1,0:T(8,128)(2,1)} %get-tuple-element.114) | data formatting | bytes 6422528
  (13 shorter events, 0.1 us)
Async XLA Ops:
  119.8 2.6 %copy-start.9 = (f32[16,512]{1,0:T(8,128)S(1)}, f32[16,512]{1,0:T(8,128)}, u32[]{:S(2)}) copy-start(f32[16,512]{1,0:T(8,128)} %get-tuple-element.65) | copy-start | bytes 98308
  119.8 2.6 %copy-start.5 = (f32[64,512]{1,0:T(8,128)S(1)}, f32[64,512]{1,0:T(8,128)}, u32[]{:S(2)}) copy-start(f32[64,512]{1,0:T(8,128)} %expand_ref.3) | copy-start | bytes 393220
  119.8 2.6 %copy-start.6 = (f32[64,512]{1,0:T(8,128)S(1)}, f32[64,512]{1,0:T(8,128)}, u32[]{:S(2)}) copy-start(f32[64,512]{1,0:T(8,128)} %contract_ref.3) | copy-start | bytes 393220
  119.8 2.6 %copy-start.7 = (f32[48,512]{1,0:T(8,128)S(1)}, f32[48,512]{1,0:T(8,128)}, u32[]{:S(2)}) copy-start(f32[48,512]{1,0:T(8,128)} %qkv_ref.3) | copy-start | bytes 294916
  119.8 2.6 %copy-start.8 = (f32[16,512]{1,0:T(8,128)S(1)}, f32[16,512]{1,0:T(8,128)}, u32[]{:S(2)}) copy-start(f32[16,512]{1,0:T(8,128)} %proj_ref.3) | copy-start | bytes 98308
  122.5 2.8 %copy-start = (bf16[16,2,192,512]{3,2,1,0:T(8,128)(2,1)S(1)}, bf16[16,2,192,512]{3,2,1,0:T(8,128)(2,1)}, u32[]{:S(2)}) copy-start(bf16[16,2,192,512]{3,2,1,0:T(8,128)(2,1)} %get-tuple-element.62) | copy-start | bytes 18874372
  125.2 66.9 %copy-start.1 = (bf16[4,196,512]{2,1,0:T(8,128)(2,1)S(1)}, bf16[4,196,512]{2,1,0:T(8,128)(2,1)}, u32[]{:S(2)}) copy-start(bf16[4,196,512]{2,1,0:T(8,128)(2,1)} %get-tuple-element.64.own_images) | copy-start | bytes 2408452
  191.4 0.7 copy-start.3
  192.2 28.4 %copy-start.2 = (f32[192,512]{1,0:T(8,128)}, f32[192,512]{1,0:T(8,128)S(1)}, u32[]{:S(2)}) copy-start(f32[192,512]{1,0:T(8,128)S(1)} %get-tuple-element.68.grads) | copy-start | bytes 1179652
  220.6 0.7 copy-start.4
  223.6 2.8 %copy-start.10 = (f32[6,512]{1,0:T(8,128)S(1)}, f32[6,512]{1,0:T(8,128)}, u32[]{:S(2)}) copy-start(f32[6,512]{1,0:T(8,128)} %param.41) | copy-start | bytes 36868
  223.6 2.8 %copy-start.11 = (f32[6,512]{1,0:T(8,128)S(1)}, f32[6,512]{1,0:T(8,128)}, u32[]{:S(2)}) copy-start(f32[6,512]{1,0:T(8,128)} %param.42) | copy-start | bytes 36868
  223.6 3.5 %copy-start.12 = (f32[169,4]{0,1:T(4,128)S(1)}, f32[169,4]{0,1:T(4,128)}, u32[]{:S(2)}) copy-start(f32[169,4]{0,1:T(4,128)} %param.47) | copy-start | bytes 8116
  223.7 3.5 %copy-start.13 = (f32[169,4]{0,1:T(4,128)S(1)}, f32[169,4]{0,1:T(4,128)}, u32[]{:S(2)}) copy-start(f32[169,4]{0,1:T(4,128)} %param.48) | copy-start | bytes 8116
  223.7 4.1 %copy-start.14 = (f32[512]{0:T(512)S(1)}, f32[512]{0:T(512)}, u32[]{:S(2)}) copy-start(f32[512]{0:T(512)} %param.45) | copy-start | bytes 6148
  223.7 4.1 %copy-start.15 = (f32[512]{0:T(512)S(1)}, f32[512]{0:T(512)}, u32[]{:S(2)}) copy-start(f32[512]{0:T(512)} %param.46) | copy-start | bytes 6148
  223.7 4.8 %copy-start.16 = (f32[2,128]{1,0:T(2,128)S(1)}, f32[2,128]{1,0:T(2,128)}, u32[]{:S(2)}) copy-start(f32[2,128]{1,0:T(2,128)} %param.43) | copy-start | bytes 3076
  223.7 4.8 %copy-start.17 = (f32[2,128]{1,0:T(2,128)S(1)}, f32[2,128]{1,0:T(2,128)}, u32[]{:S(2)}) copy-start(f32[2,128]{1,0:T(2,128)} %param.44) | copy-start | bytes 3076

commit v2 on v1

--- a/solution.py
+++ b/solution.py
@@ -196,6 +196,9 @@
     def put_grad(slice_, value):
         input_grad[slice_] = value
 
+    def two_of(body):
+        return lambda index, carry: body(2 * index + 1, body(2 * index, carry))
+
     row = lax.broadcasted_iota(jnp.int32, (batch * ROWS, 1), 0) // ROWS
     live_scale = jnp.zeros((batch * ROWS, 1), wide)
     for slice_ in range(batch):
@@ -256,7 +259,7 @@
             att_s[group, rows] = pick_heads(dot(attention.astype(low), qkv_s[8 + group, rows])).astype(low)
         return carry
 
-    lax.fori_loop(0, 8, attend, 0)
+    lax.fori_loop(0, 2, two_of(two_of(attend)), 0)
     attended = jnp.concatenate([att_s[group] for group in range(4)], axis=1)
     middle = tokens + (dot(attended, rows_of(proj_w, C)) + vectors[4:5])
     middle_s[...] = middle
@@ -337,7 +340,7 @@
         table_sum[group] += bias_grad
         return carry
 
-    lax.fori_loop(0, 8, attend_back, 0)
+    lax.fori_loop(0, 2, two_of(two_of(attend_back)), 0)
     first_in = first_s[...]
     first_grad = None
     for kind in range(3):

time: 234 us -> 226 us (0.966)
  Pallas kernels: 202 us -> 194 us
    pallas_call x1, Pallas kernels: 67.3 us -> 58.8 us  [run_layer(): pl.pallas_call(functools.partial(layer_kernel, packed, batch), out_shape=...]
where the time goes in v2:
time: 226 us
  Pallas kernels  194 us (86%)
  local copies, waits for them, and re-layouts  19.5 us (9%)
  other arithmetic  7.85 us (3%)
  matrix products  2.27 us (1%)
    pallas_call x1, Pallas kernels, muon_exchange(): pl.pallas_call(muon_kernel, out_shape=(shape, shape, jax.ShapeDtypeStruct...  64.7 us
    pallas_call x1, Pallas kernels, run_layer(): pl.pallas_call(functools.partial(layer_kernel, packed, batch), out_shape=...  58.8 us
    pallas_call x1, Pallas kernels, gather_all(): pl.pallas_call(gather_kernel, out_shape=(jax.ShapeDtypeStruct((32, rows,...  38.3 us
    pallas_call x1, Pallas kernels, newton_schulz_rows(): pl.pallas_call(ns_kernel, out_shape=(jax.ShapeDtypeStruct((4, 64, C), low...  30.1 us
    unnamed x42, local copies, waits for them, and re-layouts  13.9 us

profile of v2, /device:TPU:1, one launch (start us, length us, event | category | flops | bytes accessed | tf_op | source)
XLA Modules:
  0.0 225.5 jit_solution(12683990990463817941)
XLA Ops:
  0.7 0.7 slice.60
  1.4 0.7 slice.61
  2.1 0.1 slice_add_fusion.1
  2.1 0.1 pad_add_fusion.1
  2.2 0.1 reshape.93
  2.3 0.1 reshape.98
  2.4 0.1 compare_select_fusion
  2.5 1.3 select_maximum_fusion.2.misc_ref
  3.8 38.3 %gather_weights.1 = (bf16[32,192,512]{2,1,0:T(8,128)(2,1)}, f32[4,1,512]{2,1,0:T(1,128)}, f32[2,512]{1,0:T(2,128)}, f32[16,256]{1,0:T(8,128)}) custom-call(f32[48,512]{1,0:T(8,128)} %refs_0_.1, f32[16,512]{1,0:T(8,128)} %refs_1_.1, f32[64,512]{1,0:T(8,128)} %refs_2_.1, f32[64,512]{1,0:T(8,128)} %refs_3_.1, f32[8,512]{1,0:T(8,128)} %select_maximum_fusion.2.misc_ref), custom_call_target="tpu_custom_call" | custom-call | tf_op jit(solution)/shard_map/gather_weights/pallas_call | solution.py:722
  42.1 0.9 eq.16
  43.0 1.4 fusion.3
  44.4 0.2 add.89
  44.6 0.1 broadcast_add_fusion
  44.7 0.1 slice_bitcast_fusion.1
  44.9 1.6 fusion
  46.4 2.7 %constant_dynamic-slice_fusion.1 = (bf16[4,196,512]{2,0,1:T(4,128)(2,1)S(1)}, bf16[4,196,512]{2,0,1:T(4,128)(2,1)S(1)}) fusion(bf16[16,196,512]{2,0,1:T(8,128)(2,1)} %param.28, s32[]{:T(128)S(6)} %select_n.23, bf16[16,196,512]{2,0,1:T(8,128)(2,1)} %param.27), kind=kLoop, calls=%fused_computation.48 | loop fusion | bytes 3211268 | tf_op jit(solution)/shard_map/dynamic_slice | solution.py:1258
  49.2 1.0 copy.70.images
  50.2 1.1 copy.71.cotangent
  51.9 0.6 pad_add_fusion.2.place
  52.5 58.8 %window_layer.1 = (bf16[16,196,512]{2,1,0:T(8,128)(2,1)}, bf16[4,196,512]{2,1,0:T(8,128)(2,1)}, bf16[16,2,192,512]{3,2,1,0:T(8,128)(2,1)}, f32[16,512]{1,0:T(8,128)}, f32[4,448,112]{2,1,0:T(8,128)}) custom-call(s32[2]{0:T(128)} %pad_add_fusion.2.place, bf16[4,196,512]{2,1,0:T(8,128)(2,1)} %copy.70.images, bf16[4,196,512]{2,1,0:T(8,128)(2,1)} %copy.71.cotangent, ...), custom_call_target="tpu_custom_call" | custom-call | tf_op jit(solution)/shard_map/window_layer/pallas_call | solution.py:433
  111.3 0.0 copy-start.9
  111.3 0.0 copy-start.5
  111.3 0.0 copy-start.6
  111.3 0.0 copy-start.7
  111.4 0.0 copy-start.8
  111.4 1.4 slice_add_fusion
  112.8 0.2 reshape.96
  113.0 0.9 fusion.2
  113.9 0.0 copy-done.9
  113.9 0.0 copy-done.5
  113.9 0.0 copy-done.6
  114.0 0.0 copy-done.7
  114.0 0.0 copy-done.8
  114.0 0.0 copy-start
  114.0 2.8 %copy-done = bf16[16,2,192,512]{3,2,1,0:T(8,128)(2,1)S(1)} copy-done((bf16[16,2,192,512]{3,2,1,0:T(8,128)(2,1)S(1)}, bf16[16,2,192,512]{3,2,1,0:T(8,128)(2,1)}, u32[]{:S(2)}) %copy-start) | copy-done | bytes 6291480
  116.8 64.7 %muon_exchange.1 = (f32[192,512]{1,0:T(8,128)S(1)}, f32[192,512]{1,0:T(8,128)S(1)}, bf16[32,192,512]{2,1,0:T(8,128)(2,1)S(1)}) custom-call(bf16[4,4,2,192,512]{4,3,2,1,0:T(8,128)(2,1)S(1)} %bitcast.24, f32[48,512]{1,0:T(8,128)S(1)} %copy-done.7, f32[16,512]{1,0:T(8,128)S(1)} %copy-done.8, f32[64,512]{1,0:T(8,128)S(1)} %copy-done.5, f32[64,512]{1,0:T(8,128)S(1)} %copy-done.6), custom_call_target="tpu_custom_call" | custom-call | tf_op jit(solution)/shard_map/muon_exchange/pallas_call | solution.py:906
  181.5 0.0 copy-start.3
  181.5 0.7 copy-done.3
  182.2 0.0 copy-done.1
  182.2 30.1 %newton_schulz.1 = (bf16[4,64,512]{2,1,0:T(8,128)(2,1)S(1)}, bf16[16,196,512]{2,1,0:T(8,128)(2,1)S(1)}, f32[32,512]{1,0:T(8,128)S(1)}) custom-call(bf16[32,192,512]{2,1,0:T(8,128)(2,1)S(1)} %get-tuple-element.63.next_all, bf16[4,196,512]{2,1,0:T(8,128)(2,1)S(1)} %copy-done.1, f32[32,512]{1,0:T(8,128)S(1)} %select_maximum_fusion.1.small_ref), custom_call_target="tpu_custom_call" | custom-call | tf_op jit(solution)/shard_map/newton_schulz/pallas_call | solution.py:1077
  212.3 0.0 copy-done.2
  212.3 0.0 copy-start.4
  212.3 0.7 copy-done.4
  213.0 2.4 %update_shards.1 = (f32[48,512]{1,0:T(8,128)}, f32[16,512]{1,0:T(8,128)}, f32[64,512]{1,0:T(8,128)}, f32[64,512]{1,0:T(8,128)}, f32[48,512]{1,0:T(8,128)}, /*ind...) custom-call(f32[192,512]{1,0:T(8,128)} %copy-done.2, ...), custom_call_target="tpu_custom_call" | custom-call | tf_op jit(solution)/shard_map/update_shards/pallas_call | solution.py:1127
  215.4 0.0 copy-start.12
  215.4 0.0 copy-start.13
  215.4 0.0 copy-start.14
  215.4 0.0 copy-start.15
  215.5 0.0 copy-start.16
  215.5 0.0 copy-start.17
  215.5 2.8 %copy.67 = bf16[16,196,512]{2,0,1:T(8,128)(2,1)} copy(bf16[16,196,512]{2,1,0:T(8,128)(2,1)S(1)} %get-tuple-element.115) | data formatting | bytes 6422528
  218.2 0.0 copy-done.10
  218.2 0.0 copy-done.11
  218.2 0.6 add_divide_fusion
  218.9 0.0 copy-done.12
  218.9 0.0 copy-done.13
  218.9 0.6 add_divide_fusion.1
  219.5 0.0 copy-done.14
  219.5 0.0 copy-done.15
  219.5 0.7 add_divide_fusion.2
  220.2 0.0 copy-done.16
  220.2 0.0 copy-done.17
  220.2 0.6 add_divide_fusion.3
  220.8 4.7 %copy.66 = bf16[16,196,512]{2,0,1:T(8,128)(2,1)} copy(bf16[16,196,512]{2,1,0:T(8,128)(2,1)} %get-tuple-element.114) | data formatting | bytes 6422528
  (13 shorter events, 0.1 us)
Async XLA Ops:
  111.3 2.6 %copy-start.9 = (f32[16,512]{1,0:T(8,128)S(1)}, f32[16,512]{1,0:T(8,128)}, u32[]{:S(2)}) copy-start(f32[16,512]{1,0:T(8,128)} %get-tuple-element.65) | copy-start | bytes 98308
  111.3 2.6 %copy-start.5 = (f32[64,512]{1,0:T(8,128)S(1)}, f32[64,512]{1,0:T(8,128)}, u32[]{:S(2)}) copy-start(f32[64,512]{1,0:T(8,128)} %expand_ref.3) | copy-start | bytes 393220
  111.3 2.6 %copy-start.6 = (f32[64,512]{1,0:T(8,128)S(1)}, f32[64,512]{1,0:T(8,128)}, u32[]{:S(2)}) copy-start(f32[64,512]{1,0:T(8,128)} %contract_ref.3) | copy-start | bytes 393220
  111.3 2.6 %copy-start.7 = (f32[48,512]{1,0:T(8,128)S(1)}, f32[48,512]{1,0:T(8,128)}, u32[]{:S(2)}) copy-start(f32[48,512]{1,0:T(8,128)} %qkv_ref.3) | copy-start | bytes 294916
  111.4 2.6 %copy-start.8 = (f32[16,512]{1,0:T(8,128)S(1)}, f32[16,512]{1,0:T(8,128)}, u32[]{:S(2)}) copy-start(f32[16,512]{1,0:T(8,128)} %proj_ref.3) | copy-start | bytes 98308
  114.0 2.8 %copy-start = (bf16[16,2,192,512]{3,2,1,0:T(8,128)(2,1)S(1)}, bf16[16,2,192,512]{3,2,1,0:T(8,128)(2,1)}, u32[]{:S(2)}) copy-start(bf16[16,2,192,512]{3,2,1,0:T(8,128)(2,1)} %get-tuple-element.62) | copy-start | bytes 18874372
  116.8 65.5 %copy-start.1 = (bf16[4,196,512]{2,1,0:T(8,128)(2,1)S(1)}, bf16[4,196,512]{2,1,0:T(8,128)(2,1)}, u32[]{:S(2)}) copy-start(bf16[4,196,512]{2,1,0:T(8,128)(2,1)} %get-tuple-element.64.own_images) | copy-start | bytes 2408452
  181.5 0.7 copy-start.3
  182.2 30.1 %copy-start.2 = (f32[192,512]{1,0:T(8,128)}, f32[192,512]{1,0:T(8,128)S(1)}, u32[]{:S(2)}) copy-start(f32[192,512]{1,0:T(8,128)S(1)} %get-tuple-element.68.grads) | copy-start | bytes 1179652
  212.3 0.7 copy-start.4
  215.4 2.8 %copy-start.10 = (f32[6,512]{1,0:T(8,128)S(1)}, f32[6,512]{1,0:T(8,128)}, u32[]{:S(2)}) copy-start(f32[6,512]{1,0:T(8,128)} %param.41) | copy-start | bytes 36868
  215.4 2.8 %copy-start.11 = (f32[6,512]{1,0:T(8,128)S(1)}, f32[6,512]{1,0:T(8,128)}, u32[]{:S(2)}) copy-start(f32[6,512]{1,0:T(8,128)} %param.42) | copy-start | bytes 36868
  215.4 3.5 %copy-start.12 = (f32[169,4]{0,1:T(4,128)S(1)}, f32[169,4]{0,1:T(4,128)}, u32[]{:S(2)}) copy-start(f32[169,4]{0,1:T(4,128)} %param.47) | copy-start | bytes 8116
  215.4 3.5 %copy-start.13 = (f32[169,4]{0,1:T(4,128)S(1)}, f32[169,4]{0,1:T(4,128)}, u32[]{:S(2)}) copy-start(f32[169,4]{0,1:T(4,128)} %param.48) | copy-start | bytes 8116
  215.4 4.1 %copy-start.14 = (f32[512]{0:T(512)S(1)}, f32[512]{0:T(512)}, u32[]{:S(2)}) copy-start(f32[512]{0:T(512)} %param.45) | copy-start | bytes 6148
  215.4 4.1 %copy-start.15 = (f32[512]{0:T(512)S(1)}, f32[512]{0:T(512)}, u32[]{:S(2)}) copy-start(f32[512]{0:T(512)} %param.46) | copy-start | bytes 6148
  215.5 4.8 %copy-start.16 = (f32[2,128]{1,0:T(2,128)S(1)}, f32[2,128]{1,0:T(2,128)}, u32[]{:S(2)}) copy-start(f32[2,128]{1,0:T(2,128)} %param.43) | copy-start | bytes 3076
  215.5 4.8 %copy-start.17 = (f32[2,128]{1,0:T(2,128)S(1)}, f32[2,128]{1,0:T(2,128)}, u32[]{:S(2)}) copy-start(f32[2,128]{1,0:T(2,128)} %param.44) | copy-start | bytes 3076
